TPU v7x, 128 devices: a whole 4x4x4 slice. The times are simulated.
128 devices in a mesh: dev: 128 (over x, y, z, core).
Axes of the slice: x: 4, y: 4, z: 4, core: 2. Of those that a mesh axis runs over, the one named last changes fastest.
Arguments:
- peripheral: bfloat16 [524288, 256], P('dev'), may hold values from -6 to 6
- hubs: bfloat16 [2048, 256], P('dev'), may hold values from -6 to 6
- tiles: bfloat16 [55296, 128, 128], P('dev'), may hold values from -0.25 to 0.25
- tile_rows: int32 [55296], P('dev'), may hold values from 0 to 4111, as said below
- local_cols: int32 [38912], P('dev'), may hold values from 0 to 4111, as said below
- tile_count: int32 [128], P('dev'), may hold values from 128 to 432, as said below
- send_list: int32 [128, 128], P('dev'), may hold values from 0 to 31
- hub_place: int32 [2048], replicated, may hold values from 0 to 2047, each once
- w_in: bfloat16 [2, 256, 2048], replicated, may hold values from -0.375 to 0.375
- w_out: bfloat16 [2, 2048, 256], replicated, may hold values from -0.125 to 0.125
Outputs:
- peripheral_out: bfloat16 [524288, 256], P('dev')
- hubs_out: bfloat16 [2048, 256], P('dev')
Inputs may be any that keep to these rules, and one draw needn't show every extreme that they name: `tile_rows`: row blocks of device d's slots are hub blocks (below 16) or d's own blocks 16 + d * 32 to 16 + d * 32 + 31; slots below 128 always name an own block. `local_cols`: column blocks of device d's slots from 128 on are hub blocks or d's own blocks. `tile_count`: every device holds at least 128 live slots; some device is full in every draw.
All inputs are finite; a program needn't handle non-finite values.
Results may differ from a plain program's by a relative error of at most 0.005.
Values may be sent and summed in bfloat16 or wider, within the bound.
A program may use at most 128 MiB of HBM per device.

v0:
```python
import jax
import jax.numpy as jnp
from jax import lax
from jax.sharding import PartitionSpec as P

epsilon = 1e-06


def feed_forward(rows_in, summed, first, second):
    united = rows_in.astype(jnp.float32) + summed
    normed = (
        united * lax.rsqrt(jnp.mean(united * united, axis=-1, keepdims=True) + epsilon)
    ).astype(jnp.bfloat16)
    hidden = jnp.maximum(jnp.dot(normed, first, preferred_element_type=jnp.float32), 0.0).astype(
        jnp.bfloat16
    )
    return (united + jnp.dot(hidden, second, preferred_element_type=jnp.float32)).astype(
        jnp.bfloat16
    )


def body(
    peripheral, hubs, tiles, tile_rows, local_cols, tile_count, send_list, hub_place, w_in, w_out
):
    devices = lax.axis_size("dev")
    position = lax.axis_index("dev")
    capacity = tiles.shape[0]
    block_size = tiles.shape[1]
    width = peripheral.shape[1]
    own_count = peripheral.shape[0] // block_size
    hub_count = hub_place.shape[0] // block_size
    peri_local = peripheral.shape[0]
    targets = hub_count + own_count
    slot_index = jnp.arange(capacity, dtype=jnp.int32)
    live_slot = (slot_index < tile_count[0]).astype(jnp.float32)
    row_local = jnp.where(tile_rows < hub_count, tile_rows, tile_rows - position * own_count)
    cols_own = jnp.where(local_cols < hub_count, local_cols, local_cols - position * own_count)
    inverse = jnp.argsort(hub_place)
    peri_rows = peripheral
    hub_own = hubs
    layers = w_in.shape[0]
    for layer_index in range(layers):
        hub_full = lax.all_gather(hub_own, "dev", axis=0, tiled=True)
        hub_global = hub_full[hub_place].reshape(hub_count, block_size, width)
        own_blocks = peri_rows.reshape(own_count, block_size, width)
        outgoing = own_blocks[send_list[0]]
        empty = jnp.zeros((targets, block_size, width), jnp.float32)
        incoming = lax.all_to_all(outgoing, "dev", split_axis=0, concat_axis=0, tiled=True)
        column_table = jnp.concatenate([hub_global, own_blocks, incoming], axis=0)
        col_index = jnp.concatenate(
            [hub_count + own_count + jnp.arange(devices, dtype=jnp.int32), cols_own]
        )

        def group_step(group, carry):
            start = 0 + group * 16
            tile_group = lax.dynamic_slice_in_dim(tiles, start, 16, 0)
            col_group = lax.dynamic_slice_in_dim(col_index, start, 16, 0)
            row_group = lax.dynamic_slice_in_dim(row_local, start, 16, 0)
            live_group = lax.dynamic_slice_in_dim(live_slot, start, 16, 0)
            products = jnp.einsum(
                "tij,tjf->tif",
                tile_group,
                column_table[col_group],
                preferred_element_type=jnp.float32,
            )
            return carry.at[row_group].add(products * live_group[:, None, None])

        summed = lax.fori_loop(0, capacity // 16, group_step, empty)
        hub_part = summed[:hub_count].reshape(hub_count * block_size, width)[inverse]
        peri_sum = summed[hub_count:].reshape(peri_local, width)
        first, second = (w_in[layer_index], w_out[layer_index])
        hub_sum = lax.psum_scatter(hub_part, "dev", scatter_dimension=0, tiled=True)
        updated = feed_forward(
            jnp.concatenate([peri_rows, hub_own], axis=0),
            jnp.concatenate([peri_sum, hub_sum], axis=0),
            first,
            second,
        )
        peri_rows = updated[:peri_local]
        hub_own = updated[peri_local:]
    return (peri_rows, hub_own)


def solution(mesh):
    in_specs = (
        P("dev", None),
        P("dev", None),
        P("dev", None, None),
        P("dev"),
        P("dev"),
        P("dev"),
        P("dev", None),
        P(),
        P(),
        P(),
    )
    out_specs = (P("dev", None), P("dev", None))
    return jax.shard_map(body, mesh=mesh, in_specs=in_specs, out_specs=out_specs, check_vma=False)
```

profile of v0, /device:TPU:0, one launch (start us, length us, event | category | flops | bytes accessed | tf_op | source)
XLA Modules:
  0.0 2323.4 jit_solution(9774386568651019436)
XLA Ops:
  7.8 8.2 gather_fusion.3
  16.0 11.7 all-to-all-start
  29.2 5.0 sort.17
  34.3 132.5 %all-gather.3.cloned.1.call-done = bf16[2048,256]{1,0:T(8,128)(2,1)} async-done(((bf16[16,256]{1,0:T(8,128)(2,1)}), bf16[2048,256]{1,0:T(8,128)(2,1)}) %all-gather.3.cloned.1.call-update) | async-done | bytes 1048592 | tf_op jit(solution)/shard_map/all_gather | solution.py:43
  166.8 8.2 gather_fusion.2
  175.0 11.2 pad_maximum_fusion
  189.7 298.4 %while.26 = (s32[]{:T(128)}, f32[48,128,256]{2,1,0:T(8,128)}, s32[432]{0:T(512)S(1)}, bf16[432,128,128]{2,1,0:T(8,128)(2,1)}, s32[432]{0:T(512)S(1)}, /*index=5*...) while((s32[]{:T(128)}, f32[48,128,256]{2,1,0:T(8,128)}, ...), condition=%wide.region_2.3_spmd, body=%wide.region_0.2_spmd.sunk | while | flops 135267424 | bytes 12063527 | solution.py:68
  189.7 4.9 gather_fusion
  200.7 4.9 gather_fusion
  211.8 4.9 gather_fusion
  222.8 4.9 gather_fusion
  233.8 4.9 gather_fusion
  244.9 4.9 gather_fusion
  256.0 4.9 gather_fusion
  267.0 4.9 gather_fusion
  278.0 4.9 gather_fusion
  289.0 4.9 gather_fusion
  300.2 4.9 gather_fusion
  311.3 4.9 gather_fusion
  322.3 4.9 gather_fusion
  333.5 4.9 gather_fusion
  344.5 4.9 gather_fusion
  355.5 4.9 gather_fusion
  366.6 4.9 gather_fusion
  377.7 4.9 gather_fusion
  388.7 4.9 gather_fusion
  399.7 4.9 gather_fusion
  410.8 4.9 gather_fusion
  421.8 4.9 gather_fusion
  432.8 4.9 gather_fusion
  443.9 4.9 gather_fusion
  455.0 4.9 gather_fusion
  466.1 4.9 gather_fusion
  477.1 4.9 gather_fusion
  489.9 8.6 gather_fusion.4
  503.3 640.3 %reduce-scatter.3.cloned.1.call-done = f32[16,256]{1,0:T(8,128)} async-done(((f32[2048,256]{1,0:T(8,128)}), f32[16,256]{1,0:T(8,128)}) %reduce-scatter.3.cloned.1.call-update) | async-done | bytes 16400 | tf_op jit(solution)/shard_map/reduce_scatter | solution.py:72
  1146.6 16.8 fusion.4
  1165.1 6.8 gather_fusion.6
  1171.9 5.9 all-to-all-start.1
  1179.2 138.7 %all-gather.5.cloned.1.call-done = bf16[2048,256]{1,0:T(8,128)(2,1)} async-done(((bf16[16,256]{1,0:T(8,128)(2,1)}), bf16[2048,256]{1,0:T(8,128)(2,1)}) %all-gather.5.cloned.1.call-update) | async-done | bytes 1048592 | tf_op jit(solution)/shard_map/all_gather | solution.py:43
  1318.0 8.0 gather_fusion.5
  1326.0 11.2 pad_maximum_fusion.1
  1340.6 298.4 %while.27 = (s32[]{:T(128)}, f32[48,128,256]{2,1,0:T(8,128)}, s32[432]{0:T(512)S(1)}, bf16[432,128,128]{2,1,0:T(8,128)(2,1)}, s32[432]{0:T(512)S(1)}, /*index=5*...) while((s32[]{:T(128)}, f32[48,128,256]{2,1,0:T(8,128)}, ...), condition=%wide.region_8.9_spmd, body=%wide.region_6.8_spmd.sunk | while | flops 135267424 | bytes 12063527 | solution.py:68
  1340.7 4.9 gather_fusion.1
  1351.7 4.9 gather_fusion.1
  1640.8 8.6 gather_fusion.7
  1654.2 640.3 %reduce-scatter.5.cloned.1.call-done = f32[16,256]{1,0:T(8,128)} async-done(((f32[2048,256]{1,0:T(8,128)}), f32[16,256]{1,0:T(8,128)}) %reduce-scatter.5.cloned.1.call-update) | async-done | bytes 16400 | tf_op jit(solution)/shard_map/reduce_scatter | solution.py:72
  2297.4 15.1 fusion.5
  (346 shorter events, 488.8 us)
Async XLA Ops:
  16.0 13.2 copy-start.4
  16.0 18.2 copy-start.7
  16.0 18.2 copy-start.8
  16.0 159.0 %all-to-all-start = ((bf16[128,128,256]{2,1,0:T(8,128)(2,1)}), bf16[128,128,256]{2,1,0:T(8,128)(2,1)}, u32[]{:S(2)}, u32[]{:S(2)}) async-start(bf16[128,128,256]{2,1,0:T(8,128)(2,1)} %gather_fusion.3), calls=%async_computation | async-start | bytes 16777216 | tf_op jit(solution)/shard_map/all_to_all | solution.py:48
  27.7 139.1 %all-gather.3.cloned.1.call-start = ((), (), s32[]{:S(2)}) async-start(), calls=%async_computation.4 | async-start | bytes 1056768 | tf_op jit(solution)/shard_map/all_gather | solution.py:43
  28.4 1115.2 %reduce-scatter.3.cloned.1.call-start = ((), (), s32[]{:S(2)}) async-start(), calls=%async_computation.5 | async-start | bytes 2113536 | tf_op jit(solution)/shard_map/reduce_scatter | solution.py:72
  34.3 140.8 %copy-start = (bf16[4096,256]{1,0:T(8,128)(2,1)S(1)}, bf16[4096,256]{1,0:T(8,128)(2,1)}, u32[]{:S(2)}) copy-start(bf16[4096,256]{1,0:T(8,128)(2,1)} %param.14) | copy-start | bytes 6291460
  498.5 645.1 %copy-start.1 = (bf16[4096,256]{1,0:T(8,128)(2,1)S(1)}, bf16[4096,256]{1,0:T(8,128)(2,1)}, u32[]{:S(2)}) copy-start(bf16[4096,256]{1,0:T(8,128)(2,1)} %param.14) | copy-start | bytes 6291460
  498.5 645.1 %copy-start.3 = (bf16[16,256]{1,0:T(8,128)(2,1)S(1)}, bf16[16,256]{1,0:T(8,128)(2,1)}, u32[]{:S(2)}) copy-start(bf16[16,256]{1,0:T(8,128)(2,1)} %param.15) | copy-start | bytes 24580
  1143.6 3.0 copy-start.6
  1171.9 154.1 %all-to-all-start.1 = ((bf16[128,128,256]{2,1,0:T(8,128)(2,1)}), bf16[128,128,256]{2,1,0:T(8,128)(2,1)}, u32[]{:S(2)}, u32[]{:S(2)}) async-start(bf16[128,128,256]{2,1,0:T(8,128)(2,1)} %gather_fusion.6), calls=%async_computation.2 | async-start | bytes 16777216 | tf_op jit(solution)/shard_map/all_to_all | solution.py:48
  1177.8 140.1 %all-gather.5.cloned.1.call-start = ((), (), s32[]{:S(2)}) async-start(), calls=%async_computation.6 | async-start | bytes 1056768 | tf_op jit(solution)/shard_map/all_gather | solution.py:43
  1179.2 1115.3 %reduce-scatter.5.cloned.1.call-start = ((), (), s32[]{:S(2)}) async-start(), calls=%async_computation.7 | async-start | bytes 2113536 | tf_op jit(solution)/shard_map/reduce_scatter | solution.py:72
  1649.4 645.1 %copy-start.2 = (bf16[4112,256]{1,0:T(8,128)(2,1)S(1)}, bf16[4112,256]{1,0:T(8,128)(2,1)}, u32[]{:S(2)}) copy-start(bf16[4112,256]{1,0:T(8,128)(2,1)} %fusion.4) | copy-start | bytes 6316036
  2294.5 2.9 copy-start.5
Sparse Core Ops, SparseCore 0:
  31.3 135.4 all-gather.2
  498.6 644.9 reduce-scatter.2
  1182.0 135.9 all-gather.4
  1649.6 644.8 reduce-scatter.4
where the time goes:
time: 2330 us; the launch traced here: 2320 us
  waiting for transfers between devices  1550 us (67%)
  local copies, waits for them, and re-layouts  344 us (15%)
  other arithmetic  283 us (12%)
  matrix products  111 us (5%)
    reduce_scatter x2, waiting for transfers between devices, body(): hub_sum = lax.psum_scatter(hub_part, 'dev', scatter_dimension=0, tiled=True)  1280 us
    all_gather x2, waiting for transfers between devices, body(): hub_full = lax.all_gather(hub_own, 'dev', axis=0, tiled=True)  271 us
    gather x54, local copies, waits for them, and re-layouts, group_step(): column_table[col_group]  264 us
    scatter-add x54, other arithmetic, group_step(): return carry.at[row_group].add(products * live_group[:, None, None])  244 us
    dot_general x54, matrix products, group_step(): jnp.einsum('tij,tjf->tif', tile_group, column_table[col_group], preferred...  78.8 us
  transfers between devices with their start and end apart: 6, of which 4 were waited for; matrix products, arithmetic and copies ran while one was open for 1% of the time, Pallas kernels for 0%

commit v1 on v0

v1 whole, which is shorter than its diff:
```python
import functools
import jax
import jax.numpy as jnp
from jax import lax
from jax.sharding import PartitionSpec as P
from jax.experimental import pallas as pl
from jax.experimental.pallas import tpu as pltpu

MESH = pl.DeviceIdType.MESH
ROWS = ((0, 48), (48, 48), (96, 32))
CH = 4
epsilon = 1e-06


def coords():
    me = lax.axis_index("dev")
    return [me // 32, lax.rem(me // 8, 4), lax.rem(me // 2, 4)], lax.rem(me, 2)


def device_of(co, core):
    return ((co[0] * 4 + co[1]) * 4 + co[2]) * 2 + core


def moved(co, dim, off):
    out = list(co)
    out[dim] = lax.rem(co[dim] + off, 4)
    return out


def exchange_kernel(permute, x_ref, list_ref, hub_ref, place_ref, in_ref, near_ref, hubs_ref,
                    lists, gathered, wide, ordered, t00, t01, t02, t10, t11, t12, t20, t21, t22, s0, s1, s2, r0, r1, r2,
                    list_sem, list_send, smem_sem, ag_send, ag_recv, p2_send, p2_recv, p3_send, p3_recv, local_sem, hub_send, hub_recv):
    tabs = ((t00, t01, t02), (t10, t11, t12), (t20, t21, t22))
    stage, relay = (s0, s1, s2), (r0, r1, r2)
    co, core = coords()
    blocks = x_ref.shape[0]
    per = blocks // CH

    def to(co2, core2):
        return (device_of(co2, core2),)

    bar = pltpu.get_barrier_semaphore()
    for dim in range(3):
        for off in (1, 2, 3):
            for flip in (0, 1):
                pl.semaphore_signal(bar, inc=1, device_id=to(moved(co, dim, off), lax.rem(core + flip, 2)), device_id_type=MESH)
    pl.semaphore_signal(bar, inc=1, device_id=to(co, 1 - core), device_id_type=MESH)
    pl.semaphore_wait(bar, 19)

    def remote(src, dst, ssem, rsem, dev):
        return pltpu.make_async_remote_copy(src_ref=src, dst_ref=dst, send_sem=ssem, recv_sem=rsem, device_id=dev, device_id_type=MESH)

    def list_copy(dim, off):
        return remote(list_ref, near_ref.at[pl.ds(dim * 4 + 4 - off, 1)], list_send.at[dim, off], list_sem.at[dim, 4 - off], to(moved(co, dim, off), core))

    for dim in range(3):
        for off in (1, 2, 3):
            list_copy(dim, off).start()

    def hub_copy(step, off):
        if step == 3:
            part = gathered.at[:, :, :, core]
            return remote(part, part, hub_send.at[3, 0], hub_recv.at[3, 0], to(co, 1 - core))
        dim = 2 - step
        part = (gathered.at[co[0], co[1], co[2], core], gathered.at[co[0], co[1], :, core], gathered.at[co[0], :, :, core])[step]
        return remote(part, part, hub_send.at[step, off - 1], hub_recv.at[step, 3 - off], to(moved(co, dim, off), core))

    hub_own = pltpu.make_async_copy(hub_ref, gathered.at[co[0], co[1], co[2], core], local_sem.at[1])
    hub_own.start()
    hub_own.wait()

    def hub_start(step):
        for off in (1, 2, 3) if step < 3 else (1,):
            hub_copy(step, off).start()

    def hub_wait(step):
        for off in (1, 2, 3) if step < 3 else (1,):
            hub_copy(step, off).wait()

    hub_start(0)

    def ag_copy(p, q, direction):
        lo, n = ROWS[p]
        off = 1 if direction == 0 else 3
        seen = 4 - off
        return remote(x_ref.at[pl.ds(q * per, per), pl.ds(lo, n)], tabs[p][seen - 1].at[pl.ds(q * per, per)],
                      ag_send.at[p, q, direction], ag_recv.at[p, q, seen - 1], to(moved(co, p, off), core))

    def relay_copy(p, q):
        off = 1 if q % 2 == 0 else 3
        seen = 4 - off
        return remote(tabs[p][seen - 1].at[pl.ds(q * per, per)], tabs[p][1].at[pl.ds(q * per, per)],
                      ag_send.at[p, q, 2], ag_recv.at[p, q, 1], to(moved(co, p, off), core))

    for q in range(CH):
        for p in range(3):
            for direction in ((0, 1) if q % 2 == 0 else (1, 0)):
                ag_copy(p, q, direction).start()

    own = pltpu.make_async_copy(list_ref, near_ref.at[pl.ds(0, 1)], local_sem.at[0])
    own.start()
    own.wait()
    for dim in range(3):
        for off in (1, 2, 3):
            list_copy(dim, off).wait_recv()
    fetch = pltpu.make_async_copy(near_ref, lists, smem_sem)
    fetch.start()
    fetch.wait()

    def assemble(p, i, js):
        lo, n = ROWS[p]
        d1, d2 = (p + 1) % 3, (p + 2) % 3
        where = lax.rem(co[p] + i, 4)
        row = 0 if i == 0 else p * 4 + i
        for j in js:
            def piece(m, carry, j=j):
                k, flip = m // 2, lax.rem(m, 2)
                target = device_of(moved(moved(co, d1, j), d2, k), flip)
                b = lists[row, target]
                value = x_ref[b, lo:lo + n, :] if i == 0 else tabs[p][i - 1][b]
                stage[p][j, k, flip, where] = value
                return carry
            lax.fori_loop(0, 8, piece, 0)

    def p2_copy(p, i, j):
        d1 = (p + 1) % 3
        where = lax.rem(co[p] + i, 4)
        return remote(stage[p].at[j, :, :, where], relay[p].at[3 - j, :, :, where],
                      p2_send.at[p, i, j - 1], p2_recv.at[p, i, 3 - j], to(moved(co, d1, j), core))

    def send2(p, i):
        for j in (1, 3, 2):
            p2_copy(p, i, j).start()

    for p in range(3):
        assemble(p, 0, (1, 3, 2, 0))
    hub_wait(0)
    hub_start(1)
    for p in range(3):
        send2(p, 0)
    for q in range(CH):
        for p in range(3):
            seen = 3 if q % 2 == 0 else 1
            ag_wait(ag_recv, tabs, p, q, seen - 1, per)
            relay_copy(p, q).start()
    hub_wait(1)
    hub_start(2)
    for i in (1, 3, 2):
        if i == 2:
            hub_wait(2)
            hub_start(3)
        for p in range(3):
            for q in range(CH):
                if i == 2 or (i == 1 and q % 2 == 0) or (i == 3 and q % 2 == 1):
                    ag_wait(ag_recv, tabs, p, q, i - 1, per)
            assemble(p, i, (1, 3, 2, 0))
        for p in range(3):
            send2(p, i)

    place = ((0, 1, 2), (2, 0, 1), (1, 2, 0))

    def landing(p, s1, s2, s_core):
        lo, n = ROWS[p]
        idx = [None, None, None]
        idx[p] = slice(None)
        idx[(p + 1) % 3] = s1
        idx[(p + 2) % 3] = s2
        return in_ref.at[idx[0], idx[1], idx[2], s_core, pl.ds(lo, n)]

    def p3_copy(p, j, k, flip):
        d1, d2 = (p + 1) % 3, (p + 2) % 3
        src = stage[p].at[0, k, lax.rem(core + flip, 2)] if j == 0 else relay[p].at[j - 1, k, lax.rem(core + flip, 2)]
        s1 = lax.rem(co[d1] + j, 4)
        dst = landing(p, s1, co[d2], core)
        if k == 0 and flip == 0:
            return pltpu.make_async_copy(src, dst, local_sem.at[p * 4 + j])
        return remote(src, dst, p3_send.at[p, j, k * 2 + flip], p3_recv.at[p, j, k * 2 + flip], to(moved(co, d2, k), lax.rem(core + flip, 2)))

    def send3(p, j):
        for k in (1, 3, 2, 0):
            for flip in (0, 1):
                p3_copy(p, j, k, flip).start()

    for p in range(3):
        send3(p, 0)
    for j in (1, 3, 2):
        for p in range(3):
            for i in range(4):
                p2_wait(p2_recv, relay, p, i, j - 1)
            send3(p, j)
    hub_wait(3)
    if permute:
        wide[...] = gathered[...].astype(jnp.float32).reshape(wide.shape)

        def rows8(g, carry):
            for r in range(8):
                ordered[pl.ds(g * 8 + r, 1), :] = wide[pl.ds(place_ref[g * 8 + r], 1), :]
            return carry

        lax.fori_loop(0, wide.shape[0] // 8, rows8, 0)
        hubs_ref[...] = ordered[...].astype(jnp.bfloat16)
    else:
        hubs_ref[...] = gathered[...].reshape(hubs_ref.shape)
    for p in range(3):
        for j in range(4):
            for k in range(4):
                for flip in (0, 1):
                    if k == 0 and flip == 0:
                        p3_copy(p, j, k, flip).wait()
                    else:
                        p3_copy(p, j, k, flip).wait()
    for p in range(3):
        for q in range(CH):
            ag_copy(p, q, 0).wait_send()
            ag_copy(p, q, 1).wait_send()
            relay_copy(p, q).wait_send()
        for i in range(4):
            for j in (1, 2, 3):
                p2_copy(p, i, j).wait_send()
    for dim in range(3):
        for off in (1, 2, 3):
            list_copy(dim, off).wait_send()


def ag_wait(sem, tabs, p, q, slot, per):
    ref = tabs[p][slot].at[pl.ds(q * per, per)]
    pltpu.make_async_copy(ref, ref, sem.at[p, q, slot]).wait()


def p2_wait(sem, relay, p, i, slot):
    ref = relay[p].at[slot, :, :, 0]
    pltpu.make_async_copy(ref, ref, sem.at[p, i, slot]).wait()


def exchange(x, send_list, hubs, place, permute, cid):
    bf = jnp.bfloat16
    blocks = x.shape[0]
    hub_rows = place.shape[0]
    f32 = jnp.float32
    scratch = [pltpu.SMEM((12, 128), jnp.int32), pltpu.VMEM((4, 4, 4, 2, 16, 256), bf)]
    scratch += [pltpu.VMEM((hub_rows if permute else 8, 256), f32) for _ in range(2)]
    scratch += [pltpu.VMEM((blocks, n, 256), bf) for lo, n in ROWS for _ in range(3)]
    scratch += [pltpu.VMEM((4, 4, 2, 4, n, 256), bf) for lo, n in ROWS]
    scratch += [pltpu.VMEM((3, 4, 2, 4, n, 256), bf) for lo, n in ROWS]
    D = pltpu.SemaphoreType.DMA
    scratch += [D((3, 4)), D((3, 4)), D, D((3, CH, 3)), D((3, CH, 3)), D((3, 4, 3)), D((3, 4, 3)), D((3, 4, 8)), D((3, 4, 8)), D((12,))]
    scratch += [D((4, 3)), D((4, 3))]
    V = pl.BlockSpec(memory_space=pltpu.VMEM)
    landed, near, table = pl.pallas_call(
        functools.partial(exchange_kernel, permute),
        out_shape=(
            jax.ShapeDtypeStruct((4, 4, 4, 2, 128, 256), bf),
            jax.ShapeDtypeStruct((12, 128), jnp.int32),
            jax.ShapeDtypeStruct((hub_rows, 256), bf),
        ),
        in_specs=[V, V, V, pl.BlockSpec(memory_space=pltpu.SMEM)],
        out_specs=(pl.BlockSpec(memory_space=pltpu.HBM), V, V),
        scratch_shapes=scratch,
        compiler_params=pltpu.CompilerParams(collective_id=cid, has_side_effects=True, vmem_limit_bytes=60 * 2**20),
        name="exchange",
    )(x, send_list, hubs, place)
    return landed, table


GROUP = 16


def tiles_kernel(last, rows_ref, cols_ref, count_ref, place_ref, tiles_ref, x_ref, hubs_ref, in_ref, out_ref, *rest):
    group = pl.program_id(0)
    hub_count, own_count, remote_groups = 16, 32, 128 // GROUP
    table = rest[-1]
    count = count_ref[0]
    first = lax.axis_index("dev") == 0

    @pl.when(group == 0)
    def _():
        hub = hubs_ref[...].astype(jnp.float32)
        out_ref[0:hub_count] = jnp.where(first, hub, 0.0)
        table[0:hub_count] = hubs_ref[...]

        def own(b, carry):
            block = x_ref[b]
            out_ref[hub_count + b] = block.astype(jnp.float32)
            table[hub_count + b] = block
            return carry

        lax.fori_loop(0, own_count, own, 0)

    def add(slot, tile, block):
        row = rows_ref[slot]
        out_ref[row] = out_ref[row] + jnp.dot(tile, block, preferred_element_type=jnp.float32)

    live = jnp.clip(count - group * GROUP, 0, GROUP)

    @pl.when(group < remote_groups)
    def _():
        def step(t, carry):
            for s in range(4):
                add(group * GROUP + t * 4 + s, tiles_ref[t * 4 + s], in_ref[t * 4 + s])
            return carry

        lax.fori_loop(0, GROUP // 4, step, 0)

    def local(s):
        slot = group * GROUP + s
        add(slot, tiles_ref[s], table[cols_ref[slot - 128]])

    @pl.when((group >= remote_groups) & (live == GROUP))
    def _():
        def step(t, carry):
            for s in range(4):
                local(t * 4 + s)
            return carry

        lax.fori_loop(0, GROUP // 4, step, 0)

    @pl.when((group >= remote_groups) & (live < GROUP))
    def _():
        lax.fori_loop(0, live, lambda s, carry: (local(s), carry)[1], 0)

    if last:
        perm_ref = rest[0]

        @pl.when(group == pl.num_programs(0) - 1)
        def _():
            def rows8(g, carry):
                block = out_ref[g // 16, pl.ds(lax.rem(g, 16) * 8, 8), :]
                for r in range(8):
                    perm_ref[pl.ds(place_ref[g * 8 + r], 1), :] = block[r : r + 1]
                return carry

            lax.fori_loop(0, place_ref.shape[0] // 8, rows8, 0)


def sum_tiles(last, rows, cols, count, place, tiles, x, hubs, landed):
    capacity = tiles.shape[0]
    f32 = jnp.float32
    groups = capacity // GROUP

    def full(*shape):
        return pl.BlockSpec(shape, lambda g, *s: (0,) * len(shape))

    out_shape = [jax.ShapeDtypeStruct((48, 128, 256), f32)]
    out_specs = [full(48, 128, 256)]
    if last:
        out_shape.append(jax.ShapeDtypeStruct((2048, 256), f32))
        out_specs.append(full(2048, 256))
    return pl.pallas_call(
        functools.partial(tiles_kernel, last),
        grid_spec=pltpu.PrefetchScalarGridSpec(
            num_scalar_prefetch=4,
            grid=(groups,),
            in_specs=[
                pl.BlockSpec((GROUP, 128, 128), lambda g, rows, cols, count, place: (jnp.minimum(g, (count[0] - 1) // GROUP), 0, 0)),
                full(32, 128, 256),
                full(16, 128, 256),
                pl.BlockSpec((GROUP, 128, 256), lambda g, *s: (jnp.minimum(g, 128 // GROUP - 1), 0, 0)),
            ],
            out_specs=out_specs,
            scratch_shapes=[pltpu.VMEM((48, 128, 256), jnp.bfloat16)],
        ),
        out_shape=out_shape,
        compiler_params=pltpu.CompilerParams(dimension_semantics=("arbitrary",), vmem_limit_bytes=60 * 2**20),
        name="sum_tiles",
    )(rows, cols, count, place, tiles, x, hubs.reshape(16, 128, 256), landed.reshape(128, 128, 256))


def feed_forward(united, first, second):
    scale = lax.rsqrt(jnp.mean(united * united, axis=-1, keepdims=True) + epsilon)
    normed = (united * scale).astype(jnp.bfloat16)
    total = united
    step = 512
    for n in range(0, first.shape[1], step):
        hidden = jnp.dot(normed, first[:, n : n + step], preferred_element_type=jnp.float32)
        hidden = jnp.maximum(hidden, 0.0).astype(jnp.bfloat16)
        total = total + jnp.dot(hidden, second[n : n + step, :], preferred_element_type=jnp.float32)
    return total.astype(jnp.bfloat16)


def update_kernel(u_ref, part_ref, first_ref, second_ref, out_ref, hub_out_ref, b0, a0, b1, a1, b2, a2, b3, send, recv):
    co, core = coords()

    def to(co2, core2):
        return (device_of(co2, core2),)

    bar = pltpu.get_barrier_semaphore()
    pl.semaphore_signal(bar, inc=1, device_id=to(co, 1 - core), device_id_type=MESH)
    for dim in range(3):
        for off in (1, 2, 3):
            pl.semaphore_signal(bar, inc=1, device_id=to(moved(co, dim, off), core), device_id_type=MESH)
    pl.semaphore_wait(bar, 10)

    def remote(src, dst, ssem, rsem, dev):
        return pltpu.make_async_remote_copy(src_ref=src, dst_ref=dst, send_sem=ssem, recv_sem=rsem, device_id=dev, device_id_type=MESH)

    held = (a0, a1, a2)
    came = (b1, b2, b3)

    def copy(step, off):
        if step == 0:
            return remote(part_ref.at[0:64, 1 - core], b0, send.at[0, 0], recv.at[0, 0], to(co, 1 - core))
        dim = step - 1
        return remote(held[dim].at[lax.rem(co[dim] + off, 4)], came[dim].at[3 - off], send.at[step, off - 1], recv.at[step, 3 - off], to(moved(co, dim, off), core))

    def start(step):
        for off in (1, 2, 3) if step else (1,):
            copy(step, off).start()

    def wait(step):
        for off in (1, 2, 3) if step else (1,):
            copy(step, off).wait()

    def ffn(i, carry):
        base = 64 + i * 16
        united = u_ref[pl.ds(base, 16)].reshape(512, 256)
        out_ref[pl.ds(i * 512, 512), :] = feed_forward(united, first_ref, second_ref)
        return carry

    start(0)
    lax.fori_loop(0, 2, ffn, 0)
    wait(0)

    def add0(i, carry):
        a0[i] = (part_ref[pl.ds(i * 16, 16), core] + b0[pl.ds(i * 16, 16)]).reshape(4, 4, 16, 256)
        return carry

    lax.fori_loop(0, 4, add0, 0)
    lax.fori_loop(2, 3, ffn, 0)
    start(1)
    lax.fori_loop(3, 5, ffn, 0)
    wait(1)
    a1[...] = a0[co[0]] + b1[0] + b1[1] + b1[2]
    lax.fori_loop(5, 6, ffn, 0)
    start(2)
    lax.fori_loop(6, 7, ffn, 0)
    wait(2)
    a2[...] = a1[co[1]] + b2[0] + b2[1] + b2[2]
    lax.fori_loop(7, 8, ffn, 0)
    start(3)
    wait(3)
    hub_out_ref[...] = feed_forward(a2[co[2]] + b3[0] + b3[1] + b3[2], first_ref, second_ref)


def update(u, part, first, second, cid):
    f32, bf = jnp.float32, jnp.bfloat16
    V = pl.BlockSpec(memory_space=pltpu.VMEM)
    D = pltpu.SemaphoreType.DMA
    W = pltpu.VMEM
    return pl.pallas_call(
        update_kernel,
        out_shape=(jax.ShapeDtypeStruct((4096, 256), bf), jax.ShapeDtypeStruct((16, 256), bf)),
        in_specs=[V] * 4,
        out_specs=(V, V),
        scratch_shapes=[
            W((64, 16, 256), f32), W((4, 4, 4, 16, 256), f32),
            W((3, 4, 4, 16, 256), f32), W((4, 4, 16, 256), f32),
            W((3, 4, 16, 256), f32), W((4, 16, 256), f32),
            W((3, 16, 256), f32), D((4, 3)), D((4, 3)),
        ],
        compiler_params=pltpu.CompilerParams(collective_id=cid, has_side_effects=True, vmem_limit_bytes=60 * 2**20),
        name="update",
    )(u.reshape(192, 2, 16, 256), part.reshape(-1, 2, 16, 256), first, second)


def body(peripheral, hubs, tiles, tile_rows, local_cols, tile_count, send_list, hub_place, w_in, w_out):
    position = lax.axis_index("dev")
    hub_count, own_count = 16, 32
    rows = jnp.where(tile_rows < hub_count, tile_rows, tile_rows - position * own_count)
    cols = jnp.where(local_cols < hub_count, local_cols, local_cols - position * own_count)
    x = peripheral.reshape(own_count, 128, 256)
    hub_own = hubs
    for layer in range(2):
        landed, table = exchange(x, send_list, hub_own, hub_place, layer == 0, 2 * layer)
        sums = sum_tiles(layer == 1, rows, cols, tile_count, hub_place, tiles, x, table, landed)
        u = sums[0]
        part = sums[1] if layer == 1 else u
        new, hub_own = update(u, part, w_in[layer], w_out[layer], 2 * layer + 1)
        x = new.reshape(own_count, 128, 256)
    return new, hub_own


def solution(mesh):
    split = P("dev")
    in_specs = (split, split, split, split, split, split, split, P(), P(), P())
    return jax.shard_map(body, mesh=mesh, in_specs=in_specs, out_specs=(split, split), check_vma=False)
```

time: 2330 us -> 367 us (0.16)
  waiting for transfers between devices: 1550 us -> 0 us
  Pallas kernels: 0 us -> 353 us
  local copies, waits for them, and re-layouts: 344 us -> 8.37 us
  other arithmetic: 283 us -> 2.53 us
  matrix products: 111 us -> 0 us
    reduce_scatter x2 -> x0, waiting for transfers between devices: 1280 us -> none  [body(): hub_sum = lax.psum_scatter(hub_part, 'dev', scatter_dimension=0, tiled=True)]
    pallas_call x0 -> x6, Pallas kernels: none -> 353 us  [the longest x2 200 us: exchange(): pl.pallas_call(functools.partial(exchange_kernel, permute), out_shape=(ja...]
    gather x60 -> x0, local copies, waits for them, and re-layouts: 312 us -> none  [the longest x54 264 us: group_step(): column_table[col_group]]
    all_gather x2 -> x0, waiting for transfers between devices: 271 us -> none  [body(): hub_full = lax.all_gather(hub_own, 'dev', axis=0, tiled=True)]
    scatter-add x54 -> x0, other arithmetic: 244 us -> none  [group_step(): return carry.at[row_group].add(products * live_group[:, None, None])]
    dot_general x56 -> x0, matrix products: 111 us -> none  [the longest x54 78.8 us: group_step(): jnp.einsum('tij,tjf->tif', tile_group, column_table[col_group], preferred...]
  transfers between devices with their start and end apart: 6 -> 0, of which waited for: 4 -> 0; matrix products, arithmetic and copies ran while one was open for 1% -> 0% of each run, Pallas kernels for 0% -> 0%
where the time goes in v1:
time: 367 us; the launch traced here: 365 us
  Pallas kernels  353 us (96%)
  local copies, waits for them, and re-layouts  8.37 us (2%)
    pallas_call x2, Pallas kernels, exchange(): pl.pallas_call(functools.partial(exchange_kernel, permute), out_shape=(ja...  200 us
    pallas_call x2, Pallas kernels, update(): pl.pallas_call(update_kernel, out_shape=(jax.ShapeDtypeStruct((4096, 256)...  107 us
    pallas_call x2, Pallas kernels, sum_tiles(): pl.pallas_call(functools.partial(tiles_kernel, last), grid_spec=pltpu.Pre...  46.1 us

profile of v1, /device:TPU:0, one launch (start us, length us, event | category | flops | bytes accessed | tf_op | source)
XLA Modules:
  0.0 365.3 jit_solution(9957019720310477061)
XLA Ops:
  1.3 1.3 compare_select_fusion.1.rows_ref
  2.5 1.3 compare_select_fusion.cols_ref
  3.8 0.0 copy-start
  3.8 3.3 slice_bitcast_fusion.1
  7.1 0.0 copy-done
  7.1 1.5 slice_bitcast_fusion
  8.5 101.7 %exchange.2 = (bf16[4,4,4,2,128,256]{5,4,3,2,1,0:T(8,128)(2,1)}, s32[12,128]{1,0:T(8,128)}, bf16[2048,256]{1,0:T(8,128)(2,1)}) custom-call(bf16[32,128,256]{2,1,0:T(8,128)(2,1)} %bitcast.21, s32[1,128]{1,0:T(1,128)} %list_ref.3, bf16[16,256]{1,0:T(8,128)(2,1)} %hub_ref.1, s32[2048]{0:T(1024)} %place_ref.7), custom_call_target="tpu_custom_call" | custom-call | tf_op jit(solution)/shard_map/exchange/pallas_call | solution.py:249
  110.2 19.4 %sum_tiles.2 = f32[48,128,256]{2,1,0:T(8,128)} custom-call(s32[432]{0:T(512)} %compare_select_fusion.1.rows_ref, s32[304]{0:T(512)} %compare_select_fusion.cols_ref, s32[1]{0:T(128)S(6)} %copy.14.count_ref, s32[2048]{0:T(1024)} %place_ref.7, bf16[432,128,128]{2,1,0:T(8,128)(2,1)} %tiles_ref.3, bf16[32,128,256]{2,1,0:T(8,128)(2,1)} %bitcast.22, ...), custom_call_target="tpu_custom_call" | custom-call | tf_op jit(solution)/shard_map/sum_tiles/pallas_call | solution.py:348
  129.7 54.9 %update.2 = (bf16[4096,256]{1,0:T(8,128)(2,1)}, bf16[16,256]{1,0:T(8,128)(2,1)}) custom-call(f32[192,2,16,256]{3,2,1,0:T(8,128)} %bitcast.17, f32[192,2,16,256]{3,2,1,0:T(8,128)} %bitcast.18, bf16[256,2048]{1,0:T(8,128)(2,1)} %get-tuple-element.21.first_ref, bf16[2048,256]{1,0:T(8,128)(2,1)} %get-tuple-element.19.second_ref), custom_call_target="tpu_custom_call" | custom-call | tf_op jit(solution)/shard_map/update/pallas_call | solution.py:449
  184.6 98.3 %exchange.3 = (bf16[4,4,4,2,128,256]{5,4,3,2,1,0:T(8,128)(2,1)}, s32[12,128]{1,0:T(8,128)}, bf16[2048,256]{1,0:T(8,128)(2,1)}) custom-call(bf16[32,128,256]{2,1,0:T(8,128)(2,1)} %bitcast.23, s32[1,128]{1,0:T(1,128)} %list_ref.3, bf16[16,256]{1,0:T(8,128)(2,1)} %get-tuple-element.13.hub_ref, s32[2048]{0:T(1024)} %place_ref.7), custom_call_target="tpu_custom_call" | custom-call | tf_op jit(solution)/shard_map/exchange/pallas_call | solution.py:249
  282.9 26.6 %sum_tiles.3 = (f32[48,128,256]{2,1,0:T(8,128)}, f32[2048,256]{1,0:T(8,128)}) custom-call(s32[432]{0:T(512)} %compare_select_fusion.1.rows_ref, s32[304]{0:T(512)} %compare_select_fusion.cols_ref, s32[1]{0:T(128)S(6)} %copy.14.count_ref, s32[2048]{0:T(1024)} %place_ref.7, bf16[432,128,128]{2,1,0:T(8,128)(2,1)} %tiles_ref.3, bf16[32,128,256]{2,1,0:T(8,128)(2,1)} %bitcast.24, ...), custom_call_target="tpu_custom_call" | custom-call | tf_op jit(solution)/shard_map/sum_tiles/pallas_call | solution.py:348
  309.6 52.1 %update.3 = (bf16[4096,256]{1,0:T(8,128)(2,1)}, bf16[16,256]{1,0:T(8,128)(2,1)}) custom-call(f32[192,2,16,256]{3,2,1,0:T(8,128)} %bitcast.25, f32[64,2,16,256]{3,2,1,0:T(8,128)} %bitcast.26, bf16[256,2048]{1,0:T(8,128)(2,1)} %get-tuple-element.20.first_ref, bf16[2048,256]{1,0:T(8,128)(2,1)} %get-tuple-element.18.second_ref), custom_call_target="tpu_custom_call" | custom-call | tf_op jit(solution)/shard_map/update/pallas_call | solution.py:449
  361.7 0.0 copy-start.1
  361.7 3.0 copy.15
  364.7 0.0 copy-done.1
  364.7 0.6 copy.16
Async XLA Ops:
  3.8 3.3 copy-start
  361.7 3.1 copy-start.1

commit v2 on v1

v2 whole, which is shorter than its diff:
```python
import functools
import jax
import jax.numpy as jnp
from jax import lax
from jax.sharding import PartitionSpec as P
from jax.experimental import pallas as pl
from jax.experimental.pallas import tpu as pltpu

MESH = pl.DeviceIdType.MESH
ROWS = ((0, 48), (48, 48), (96, 32))
epsilon = 1e-06


def coords():
    me = lax.axis_index("dev")
    return [me // 32, lax.rem(me // 8, 4), lax.rem(me // 2, 4)], lax.rem(me, 2)


def device_of(co, core):
    return ((co[0] * 4 + co[1]) * 4 + co[2]) * 2 + core


def moved(co, dim, off):
    out = list(co)
    out[dim] = lax.rem(co[dim] + off, 4)
    return out


def exchange_kernel(fused, CH, *refs):
    if fused:
        u_ref, lists, w1_ref, w2_ref, in_ref, hubs_ref, x_ref = refs[:7]
        first_ref, second_ref, hidden_ref, normed_ref, w_sem = refs[7:12]
        sum_refs = refs[12:23]
        refs = refs[23:]
    else:
        x_ref, list_ref, hub_ref, place_ref, in_ref, hubs_ref, near_ref, lists, wide, ordered = refs[:10]
        refs = refs[10:]
    exchange_steps(fused, CH, locals(), *refs)


def exchange_steps(fused, CH, given, gathered, t00, t01, t02, t10, t11, t12, t20, t21, t22, s0, s1, s2, r0, r1, r2,
                    list_sem, list_send, smem_sem, ag_send, ag_recv, p2_send, p2_recv, p3_send, p3_recv, local_sem, hub_send, hub_recv):
    x_ref, in_ref, hubs_ref, lists = given["x_ref"], given["in_ref"], given["hubs_ref"], given["lists"]
    if fused:
        weights = load_weights(given["w1_ref"], given["w2_ref"], given["first_ref"], given["second_ref"], given["w_sem"], 0)
    else:
        list_ref, hub_ref, place_ref, near_ref = given["list_ref"], given["hub_ref"], given["place_ref"], given["near_ref"]
    tabs = ((t00, t01, t02), (t10, t11, t12), (t20, t21, t22))
    stage, relay = (s0, s1, s2), (r0, r1, r2)
    co, core = coords()
    blocks = x_ref.shape[0]
    per = blocks // CH

    def to(co2, core2):
        return (device_of(co2, core2),)

    bar = pltpu.get_barrier_semaphore()
    for dim in range(3):
        for off in (1, 2, 3):
            for flip in (0, 1):
                pl.semaphore_signal(bar, inc=1, device_id=to(moved(co, dim, off), lax.rem(core + flip, 2)), device_id_type=MESH)
    pl.semaphore_signal(bar, inc=1, device_id=to(co, 1 - core), device_id_type=MESH)
    pl.semaphore_wait(bar, 19)

    def remote(src, dst, ssem, rsem, dev):
        return pltpu.make_async_remote_copy(src_ref=src, dst_ref=dst, send_sem=ssem, recv_sem=rsem, device_id=dev, device_id_type=MESH)

    def list_copy(dim, off):
        return remote(list_ref, near_ref.at[pl.ds(dim * 4 + 4 - off, 1)], list_send.at[dim, off], list_sem.at[dim, 4 - off], to(moved(co, dim, off), core))

    def hub_copy(step, off):
        if step == 3:
            part = gathered.at[:, :, :, core]
            return remote(part, part, hub_send.at[3, 0], hub_recv.at[3, 0], to(co, 1 - core))
        dim = 2 - step
        part = (gathered.at[co[0], co[1], co[2], core], gathered.at[co[0], co[1], :, core], gathered.at[co[0], :, :, core])[step]
        return remote(part, part, hub_send.at[step, off - 1], hub_recv.at[step, 3 - off], to(moved(co, dim, off), core))

    def hub_start(step):
        for off in (1, 2, 3) if step < 3 else (1,):
            hub_copy(step, off).start()

    def hub_wait(step):
        for off in (1, 2, 3) if step < 3 else (1,):
            hub_copy(step, off).wait()

    def ag_copy(p, q, direction):
        lo, n = ROWS[p]
        off = 1 if direction == 0 else 3
        seen = 4 - off
        return remote(x_ref.at[pl.ds(q * per, per), pl.ds(lo, n)], tabs[p][seen - 1].at[pl.ds(q * per, per)],
                      ag_send.at[p, q, direction], ag_recv.at[p, q, seen - 1], to(moved(co, p, off), core))

    def relay_copy(p, q):
        off = 1 if q % 2 == 0 else 3
        seen = 4 - off
        return remote(tabs[p][seen - 1].at[pl.ds(q * per, per)], tabs[p][1].at[pl.ds(q * per, per)],
                      ag_send.at[p, q, 2], ag_recv.at[p, q, 1], to(moved(co, p, off), core))

    def ag_start(q):
        for p in range(3):
            for direction in (0, 1) if q % 2 == 0 else (1, 0):
                ag_copy(p, q, direction).start()

    def relay_on(q):
        for p in range(3):
            ag_wait(ag_recv, tabs, p, q, 2 if q % 2 == 0 else 0, per)
            relay_copy(p, q).start()

    def assemble(p, i, js):
        lo, n = ROWS[p]
        d1, d2 = (p + 1) % 3, (p + 2) % 3
        where = lax.rem(co[p] + i, 4)
        row = 0 if i == 0 else p * 4 + i
        for j in js:
            def piece(m, carry, j=j):
                k, flip = m // 2, lax.rem(m, 2)
                target = device_of(moved(moved(co, d1, j), d2, k), flip)
                b = lists[row, target]
                value = x_ref[b, lo:lo + n, :] if i == 0 else tabs[p][i - 1][b]
                stage[p][j, k, flip, where] = value
                return carry
            lax.fori_loop(0, 8, piece, 0)

    def p2_copy(p, i, j):
        d1 = (p + 1) % 3
        where = lax.rem(co[p] + i, 4)
        return remote(stage[p].at[j, :, :, where], relay[p].at[3 - j, :, :, where],
                      p2_send.at[p, i, j - 1], p2_recv.at[p, i, 3 - j], to(moved(co, d1, j), core))

    def send2(p, i):
        for j in (1, 3, 2):
            p2_copy(p, i, j).start()

    def pass_on(i):
        for p in range(3):
            for q in range(CH):
                if i == 2 or (i == 1 and q % 2 == 0) or (i == 3 and q % 2 == 1):
                    ag_wait(ag_recv, tabs, p, q, i - 1, per)
            assemble(p, i, (1, 3, 2, 0))
            if p:
                send2(p - 1, i)
        send2(2, i)

    place = ((0, 1, 2), (2, 0, 1), (1, 2, 0))

    def landing(p, s1, s2, s_core):
        lo, n = ROWS[p]
        idx = [None, None, None]
        idx[p] = slice(None)
        idx[(p + 1) % 3] = s1
        idx[(p + 2) % 3] = s2
        return in_ref.at[idx[0], idx[1], idx[2], s_core, pl.ds(lo, n)]

    def p3_copy(p, j, k, flip):
        d1, d2 = (p + 1) % 3, (p + 2) % 3
        src = stage[p].at[0, k, lax.rem(core + flip, 2)] if j == 0 else relay[p].at[j - 1, k, lax.rem(core + flip, 2)]
        s1 = lax.rem(co[d1] + j, 4)
        dst = landing(p, s1, co[d2], core)
        if k == 0 and flip == 0:
            return pltpu.make_async_copy(src, dst, local_sem.at[p * 4 + j])
        return remote(src, dst, p3_send.at[p, j, k * 2 + flip], p3_recv.at[p, j, k * 2 + flip], to(moved(co, d2, k), lax.rem(core + flip, 2)))

    def send3(p, j):
        for k in (1, 3, 2, 0):
            for flip in (0, 1):
                p3_copy(p, j, k, flip).start()

    def finish(j):
        for p in range(3):
            for i in range(4):
                p2_wait(p2_recv, relay, p, i, j - 1)
            send3(p, j)

    def own_pass():
        for p in range(3):
            assemble(p, 0, (1, 3, 2, 0))
            if fused and p == 0:
                ag_start(CH - 1)
            if p:
                send2(p - 1, 0)
        send2(2, 0)

    if fused:
        sums = HubSum(co, core, remote, to, u_ref := given["u_ref"], *given["sum_refs"])
        sums.start(0)
        weights()
        first_ref, second_ref = given["first_ref"], given["second_ref"]
        size = 4096 // CH
        for q in range(CH):
            update_rows(u_ref, x_ref, q, size, first_ref, second_ref, given["hidden_ref"], given["normed_ref"])
            if q >= 1:
                ag_start(q - 1)
            if q == 2:
                sums.wait(0)
                sums.add(0)
            if q == 3:
                sums.start(1)
            if q >= 4:
                relay_on(q - 4)
        own_pass()
        sums.wait(1)
        sums.add(1)
        for q in range(CH - 4, CH):
            relay_on(q)
            if q == CH - 3:
                sums.start(2)
        pass_on(1)
        sums.wait(2)
        sums.add(2)
        pass_on(3)
        sums.start(3)
        pass_on(2)
        sums.wait(3)
        gathered[co[0], co[1], co[2], core] = feed_forward(sums.result(), first_ref, second_ref)
        for p in range(3):
            send3(p, 0)
        hub_start(0)
        finish(1)
        hub_wait(0)
        hub_start(1)
        finish(3)
        hub_wait(1)
        hub_start(2)
        finish(2)
        hub_wait(2)
        hub_start(3)
    else:
        for dim in range(3):
            for off in (1, 2, 3):
                list_copy(dim, off).start()
        hub_own = pltpu.make_async_copy(hub_ref, gathered.at[co[0], co[1], co[2], core], local_sem.at[1])
        hub_own.start()
        hub_own.wait()
        hub_start(0)
        for q in range(CH):
            ag_start(q)
        own = pltpu.make_async_copy(list_ref, near_ref.at[pl.ds(0, 1)], local_sem.at[0])
        own.start()
        own.wait()
        for dim in range(3):
            for off in (1, 2, 3):
                list_copy(dim, off).wait_recv()
        fetch = pltpu.make_async_copy(near_ref, lists, smem_sem)
        fetch.start()
        fetch.wait()
        own_pass()
        hub_wait(0)
        hub_start(1)
        for q in range(CH):
            relay_on(q)
        hub_wait(1)
        hub_start(2)
        pass_on(1)
        pass_on(3)
        hub_wait(2)
        hub_start(3)
        pass_on(2)
        for p in range(3):
            send3(p, 0)
        for j in (1, 3, 2):
            finish(j)
    hub_wait(3)
    if not fused:
        wide, ordered = given["wide"], given["ordered"]
        wide[...] = gathered[...].astype(jnp.float32).reshape(wide.shape)

        def rows8(g, carry):
            for r in range(8):
                ordered[pl.ds(g * 8 + r, 1), :] = wide[pl.ds(place_ref[g * 8 + r], 1), :]
            return carry

        lax.fori_loop(0, wide.shape[0] // 8, rows8, 0)
        hubs_ref[...] = ordered[...].astype(jnp.bfloat16)
    else:
        hubs_ref[...] = gathered[...].reshape(hubs_ref.shape)
    for p in range(3):
        for j in range(4):
            for k in range(4):
                for flip in (0, 1):
                    if k == 0 and flip == 0:
                        p3_copy(p, j, k, flip).wait()
                    else:
                        p3_copy(p, j, k, flip).wait()
    for p in range(3):
        for q in range(CH):
            ag_copy(p, q, 0).wait_send()
            ag_copy(p, q, 1).wait_send()
            relay_copy(p, q).wait_send()
        for i in range(4):
            for j in (1, 2, 3):
                p2_copy(p, i, j).wait_send()
    if not fused:
        for dim in range(3):
            for off in (1, 2, 3):
                list_copy(dim, off).wait_send()


def ag_wait(sem, tabs, p, q, slot, per):
    ref = tabs[p][slot].at[pl.ds(q * per, per)]
    pltpu.make_async_copy(ref, ref, sem.at[p, q, slot]).wait()


def p2_wait(sem, relay, p, i, slot):
    ref = relay[p].at[slot, :, :, 0]
    pltpu.make_async_copy(ref, ref, sem.at[p, i, slot]).wait()


def load_weights(w1_ref, w2_ref, first_ref, second_ref, sem, layer):
    copies = [
        pltpu.make_async_copy(w1_ref.at[layer], first_ref, sem.at[0]),
        pltpu.make_async_copy(w2_ref.at[layer], second_ref, sem.at[1]),
    ]
    for copy in copies:
        copy.start()

    def wait():
        for copy in copies:
            copy.wait()

    return wait


class HubSum:
    orders = ((0, 1, 2), (1, 2, 0))

    def __init__(self, co, core, remote, to, part, b0, a0, b1a, b1b, a1, b2a, b2b, a2, b3, send, recv):
        self.co, self.core, self.remote, self.to, self.part = co, core, remote, to, part
        self.b0, self.a0, self.a1, self.a2 = b0, a0, a1, a2
        self.came = ((b1a, b1b), (b2a, b2b), (b3.at[0], b3.at[1]))
        self.b3, self.send, self.recv = b3, send, recv

    def source(self, step, p, at):
        if step == 1:
            rows = pl.ds(p * 8, 8)
            return self.a0.at[at, :, :, rows] if p == 0 else self.a0.at[:, at, :, rows]
        if step == 2:
            return self.a1.at[p, at] if p == 0 else self.a1.at[p, :, at]
        return self.a2.at[p, at]

    def copies(self, step):
        if step == 0:
            return [self.remote(self.part.at[0:64, 1 - self.core], self.b0, self.send.at[0, 0, 0], self.recv.at[0, 0, 0], self.to(self.co, 1 - self.core))]
        out = []
        for p, order in enumerate(self.orders):
            dim = order[step - 1]
            for off in (1, 2, 3):
                src = self.source(step, p, lax.rem(self.co[dim] + off, 4))
                out.append(self.remote(src, self.came[step - 1][p].at[3 - off], self.send.at[step, p, off - 1], self.recv.at[step, p, 3 - off], self.to(moved(self.co, dim, off), self.core)))
        return out

    def start(self, step):
        for copy in self.copies(step):
            copy.start()

    def wait(self, step):
        for copy in self.copies(step):
            copy.wait()

    def add(self, step):
        if step == 0:

            def add0(i, carry):
                self.a0[i] = (self.part[pl.ds(i * 16, 16), self.core] + self.b0[pl.ds(i * 16, 16)]).reshape(4, 4, 16, 256)
                return carry

            lax.fori_loop(0, 4, add0, 0)
            return
        held = self.a1 if step == 1 else self.a2
        for p, order in enumerate(self.orders):
            came = self.came[step - 1][p]
            at = self.co[order[step - 1]]
            if step == 1:
                own = self.a0[at, :, :, p * 8 : p * 8 + 8] if p == 0 else self.a0[:, at, :, p * 8 : p * 8 + 8]
            else:
                own = self.a1[p, at] if p == 0 else self.a1[p, :, at]
            held[p] = own + came[0] + came[1] + came[2]

    def result(self):
        rows = []
        for p, order in enumerate(self.orders):
            rows.append(self.a2[p, self.co[order[2]]] + self.b3[p, 0] + self.b3[p, 1] + self.b3[p, 2])
        return jnp.concatenate(rows, axis=0)


def sum_scratch():
    W, f32, D = pltpu.VMEM, jnp.float32, pltpu.SemaphoreType.DMA
    return [
        W((64, 16, 256), f32), W((4, 4, 4, 16, 256), f32),
        W((3, 4, 4, 8, 256), f32), W((3, 4, 4, 8, 256), f32), W((2, 4, 4, 8, 256), f32),
        W((3, 4, 8, 256), f32), W((3, 4, 8, 256), f32), W((2, 4, 8, 256), f32),
        W((2, 3, 8, 256), f32), D((4, 2, 3)), D((4, 2, 3)),
    ]


def weight_scratch(size):
    bf = jnp.bfloat16
    return [pltpu.VMEM((256, 2048), bf), pltpu.VMEM((2048, 256), bf), pltpu.VMEM((size, 2048), bf), pltpu.VMEM((size, 256), bf), pltpu.SemaphoreType.DMA((2,))]


def update_rows(u_ref, x_ref, q, size, first, second, hidden_ref, normed_ref):
    def united():
        return u_ref[pl.ds(64 + q * (size // 32), size // 32)].reshape(size, 256)

    u = united()
    normed_ref[...] = (u * lax.rsqrt(jnp.mean(u * u, axis=-1, keepdims=True) + epsilon)).astype(jnp.bfloat16)
    for n in range(0, 2048, 256):
        value = jnp.dot(normed_ref[...], first[:, n : n + 256], preferred_element_type=jnp.float32)
        hidden_ref[:, n : n + 256] = jnp.maximum(value, 0.0).astype(jnp.bfloat16)
    total = united() + jnp.dot(hidden_ref[...], second[...], preferred_element_type=jnp.float32)
    x_ref[pl.ds(q * (size // 128), size // 128)] = total.astype(jnp.bfloat16).reshape(size // 128, 128, 256)


def route_scratch(chunks):
    bf, D = jnp.bfloat16, pltpu.SemaphoreType.DMA
    scratch = [pltpu.VMEM((4, 4, 4, 2, 16, 256), bf)]
    scratch += [pltpu.VMEM((32, n, 256), bf) for lo, n in ROWS for _ in range(3)]
    scratch += [pltpu.VMEM((4, 4, 2, 4, n, 256), bf) for lo, n in ROWS]
    scratch += [pltpu.VMEM((3, 4, 2, 4, n, 256), bf) for lo, n in ROWS]
    scratch += [D((3, 4)), D((3, 4)), D, D((3, chunks, 3)), D((3, chunks, 3)), D((3, 4, 3)), D((3, 4, 3)), D((3, 4, 8)), D((3, 4, 8)), D((12,))]
    return scratch + [D((4, 3)), D((4, 3))]


def exchange(x, send_list, hubs, place):
    bf, f32 = jnp.bfloat16, jnp.float32
    V = pl.BlockSpec(memory_space=pltpu.VMEM)
    return pl.pallas_call(
        functools.partial(exchange_kernel, False, 4),
        out_shape=(
            jax.ShapeDtypeStruct((4, 4, 4, 2, 128, 256), bf),
            jax.ShapeDtypeStruct((2048, 256), bf),
            jax.ShapeDtypeStruct((12, 128), jnp.int32),
        ),
        in_specs=[V, V, V, pl.BlockSpec(memory_space=pltpu.SMEM)],
        out_specs=(pl.BlockSpec(memory_space=pltpu.HBM), V, V),
        scratch_shapes=[pltpu.SMEM((12, 128), jnp.int32), pltpu.VMEM((2048, 256), f32), pltpu.VMEM((2048, 256), f32)] + route_scratch(4),
        compiler_params=pltpu.CompilerParams(collective_id=0, has_side_effects=True, vmem_limit_bytes=60 * 2**20),
        name="exchange",
    )(x, send_list, hubs, place)


def update_exchange(u, near, w_in, w_out):
    bf = jnp.bfloat16
    V, A = pl.BlockSpec(memory_space=pltpu.VMEM), pl.BlockSpec(memory_space=pl.ANY)
    return pl.pallas_call(
        functools.partial(exchange_kernel, True, 8),
        out_shape=(
            jax.ShapeDtypeStruct((4, 4, 4, 2, 128, 256), bf),
            jax.ShapeDtypeStruct((2048, 256), bf),
            jax.ShapeDtypeStruct((32, 128, 256), bf),
        ),
        in_specs=[V, pl.BlockSpec(memory_space=pltpu.SMEM), A, A],
        out_specs=(pl.BlockSpec(memory_space=pltpu.HBM), V, V),
        scratch_shapes=weight_scratch(512) + sum_scratch() + route_scratch(8),
        compiler_params=pltpu.CompilerParams(collective_id=1, has_side_effects=True, vmem_limit_bytes=60 * 2**20),
        name="update_exchange",
    )(u.reshape(192, 2, 16, 256), near, w_in, w_out)


GROUP = 64
BATCH = 16


def tiles_kernel(last, rows_ref, cols_ref, count_ref, place_ref, tiles_ref, x_ref, hubs_ref, in_ref, out_ref, *rest):
    group = pl.program_id(0)
    hub_count, own_count, remote_groups = 16, 32, 128 // GROUP
    table = rest[-1]
    count = count_ref[0]
    position = lax.axis_index("dev")

    def near(block):
        return jnp.where(block < hub_count, block, block - position * own_count)

    @pl.when(group == 0)
    def _():
        def hub(b, carry):
            block = hubs_ref[b]
            out_ref[b] = jnp.where(position == 0, block.astype(jnp.float32), 0.0)
            table[b] = block
            return carry

        lax.fori_loop(0, hub_count, hub, 0)

        def own(b, carry):
            block = x_ref[b]
            out_ref[hub_count + b] = block.astype(jnp.float32)
            table[hub_count + b] = block
            return carry

        lax.fori_loop(0, own_count, own, 0)

    def add(items):
        products = [jnp.dot(tile, block, preferred_element_type=jnp.float32) for slot, tile, block in items]
        for (slot, tile, block), product in zip(items, products):
            row = near(rows_ref[slot])
            out_ref[row] = out_ref[row] + product

    live = jnp.clip(count - group * GROUP, 0, GROUP)

    @pl.when(group < remote_groups)
    def _():
        def step(t, carry):
            add([(group * GROUP + t * BATCH + s, tiles_ref[t * BATCH + s], in_ref[t * BATCH + s]) for s in range(BATCH)])
            return carry

        lax.fori_loop(0, GROUP // BATCH, step, 0)

    @pl.when(group >= remote_groups)
    def _():
        def local(s):
            slot = group * GROUP + s
            return slot, tiles_ref[s], table[near(cols_ref[slot - 128])]

        def step(t, carry):
            add([local(t * BATCH + s) for s in range(BATCH)])
            return carry

        full = live // BATCH
        lax.fori_loop(0, full, step, 0)
        lax.fori_loop(full * BATCH, live, lambda s, carry: (add([local(s)]), carry)[1], 0)

    if last:
        perm_ref = rest[0]

        @pl.when(group == pl.num_programs(0) - 1)
        def _():
            def rows32(g, carry):
                block = out_ref[g // 4, pl.ds(lax.rem(g, 4) * 32, 32), :]
                for r in range(32):
                    perm_ref[pl.ds(place_ref[g * 32 + r], 1), :] = block[r : r + 1]
                return carry

            lax.fori_loop(0, place_ref.shape[0] // 32, rows32, 0)


def sum_tiles(last, rows, cols, count, place, tiles, x, hubs, landed):
    capacity = tiles.shape[0]
    f32 = jnp.float32
    groups = -(-capacity // GROUP)

    def full(*shape):
        return pl.BlockSpec(shape, lambda g, *s: (0,) * len(shape))

    out_shape = [jax.ShapeDtypeStruct((48, 128, 256), f32)]
    out_specs = [full(48, 128, 256)]
    if last:
        out_shape.append(jax.ShapeDtypeStruct((2048, 256), f32))
        out_specs.append(full(2048, 256))
    return pl.pallas_call(
        functools.partial(tiles_kernel, last),
        grid_spec=pltpu.PrefetchScalarGridSpec(
            num_scalar_prefetch=4,
            grid=(groups,),
            in_specs=[
                pl.BlockSpec((GROUP, 128, 128), lambda g, rows, cols, count, place: (jnp.minimum(g, (count[0] - 1) // GROUP), 0, 0)),
                full(32, 128, 256),
                full(16, 128, 256),
                pl.BlockSpec((GROUP, 128, 256), lambda g, *s: (jnp.minimum(g, 128 // GROUP - 1), 0, 0)),
            ],
            out_specs=out_specs,
            scratch_shapes=[pltpu.VMEM((48, 128, 256), jnp.bfloat16)],
        ),
        out_shape=out_shape,
        compiler_params=pltpu.CompilerParams(dimension_semantics=("arbitrary",), vmem_limit_bytes=60 * 2**20),
        name="sum_tiles",
    )(rows, cols, count, place, tiles, x, hubs.reshape(16, 128, 256), landed.reshape(128, 128, 256))


def feed_forward(united, first, second):
    scale = lax.rsqrt(jnp.mean(united * united, axis=-1, keepdims=True) + epsilon)
    normed = (united * scale).astype(jnp.bfloat16)
    total = united
    step = 512
    for n in range(0, first.shape[1], step):
        hidden = jnp.dot(normed, first[:, n : n + step], preferred_element_type=jnp.float32)
        hidden = jnp.maximum(hidden, 0.0).astype(jnp.bfloat16)
        total = total + jnp.dot(hidden, second[n : n + step, :], preferred_element_type=jnp.float32)
    return total.astype(jnp.bfloat16)


def update_kernel(u_ref, part_ref, w1_ref, w2_ref, out_ref, hub_out_ref, first_ref, second_ref, hidden_ref, normed_ref, w_sem, *sum_refs):
    weights = load_weights(w1_ref, w2_ref, first_ref, second_ref, w_sem, 1)
    co, core = coords()

    def to(co2, core2):
        return (device_of(co2, core2),)

    bar = pltpu.get_barrier_semaphore()
    pl.semaphore_signal(bar, inc=1, device_id=to(co, 1 - core), device_id_type=MESH)
    for dim in range(3):
        for off in (1, 2, 3):
            pl.semaphore_signal(bar, inc=1, device_id=to(moved(co, dim, off), core), device_id_type=MESH)
    pl.semaphore_wait(bar, 10)

    def remote(src, dst, ssem, rsem, dev):
        return pltpu.make_async_remote_copy(src_ref=src, dst_ref=dst, send_sem=ssem, recv_sem=rsem, device_id=dev, device_id_type=MESH)

    sums = HubSum(co, core, remote, to, part_ref, *sum_refs)
    sums.start(0)
    weights()
    size = hidden_ref.shape[0]
    for q in range(4096 // size):
        update_rows(u_ref, out_ref, q, size, first_ref, second_ref, hidden_ref, normed_ref)
        if q == 1:
            sums.wait(0)
            sums.add(0)
        if q == 2:
            sums.start(1)
        if q == 5:
            sums.wait(1)
            sums.add(1)
        if q == 6:
            sums.start(2)
    sums.wait(2)
    sums.add(2)
    sums.start(3)
    sums.wait(3)
    hub_out_ref[...] = feed_forward(sums.result(), first_ref, second_ref)


def update(u, part, w_in, w_out):
    bf = jnp.bfloat16
    V, A = pl.BlockSpec(memory_space=pltpu.VMEM), pl.BlockSpec(memory_space=pl.ANY)
    return pl.pallas_call(
        update_kernel,
        out_shape=(jax.ShapeDtypeStruct((32, 128, 256), bf), jax.ShapeDtypeStruct((16, 256), bf)),
        in_specs=[V, V, A, A],
        out_specs=(V, V),
        scratch_shapes=weight_scratch(512) + sum_scratch(),
        compiler_params=pltpu.CompilerParams(collective_id=2, has_side_effects=True, vmem_limit_bytes=60 * 2**20),
        name="update",
    )(u.reshape(192, 2, 16, 256), part.reshape(-1, 2, 16, 256), w_in, w_out)


def body(peripheral, hubs, tiles, tile_rows, local_cols, tile_count, send_list, hub_place, w_in, w_out):
    x = peripheral.reshape(-1, 128, 256)
    landed, table, near = exchange(x, send_list, hubs, hub_place)
    (u,) = sum_tiles(False, tile_rows, local_cols, tile_count, hub_place, tiles, x, table, landed)
    landed, table, x = update_exchange(u, near, w_in, w_out)
    u, part = sum_tiles(True, tile_rows, local_cols, tile_count, hub_place, tiles, x, table, landed)
    new, hub_new = update(u, part, w_in, w_out)
    return new.reshape(peripheral.shape), hub_new


def solution(mesh):
    split = P("dev")
    in_specs = (split, split, split, split, split, split, split, P(), P(), P())
    return jax.shard_map(body, mesh=mesh, in_specs=in_specs, out_specs=(split, split), check_vma=False)
```

time: 367 us -> 299 us (0.81)
  Pallas kernels: 353 us -> 295 us
  local copies, waits for them, and re-layouts: 8.37 us -> 3.65 us
    pallas_call x4 -> x3, Pallas kernels: 307 us -> 265 us  [the longest x1 121 us: update_exchange(): pl.pallas_call(functools.partial(exchange_kernel, True, 8), out_shape=(ja...]
    pallas_call x2, Pallas kernels: 46.1 us -> 30.5 us  [sum_tiles(): pl.pallas_call(functools.partial(tiles_kernel, last), grid_spec=pltpu.Pre...]
    squeeze x2 -> x0, local copies, waits for them, and re-layouts: 4.71 us -> none  [body(): new, hub_own = update(u, part, w_in[layer], w_out[layer], 2 * layer + 1)]
where the time goes in v2:
time: 299 us; the launch traced here: 300 us
  Pallas kernels  295 us (99%)
  local copies, waits for them, and re-layouts  3.65 us (1%)
    pallas_call x1, Pallas kernels, update_exchange(): pl.pallas_call(functools.partial(exchange_kernel, True, 8), out_shape=(ja...  121 us
    pallas_call x1, Pallas kernels, exchange(): pl.pallas_call(functools.partial(exchange_kernel, False, 4), out_shape=(j...  105 us
    pallas_call x1, Pallas kernels, update(): pl.pallas_call(update_kernel, out_shape=(jax.ShapeDtypeStruct((32, 128, 2...  39.6 us
    pallas_call x2, Pallas kernels, sum_tiles(): pl.pallas_call(functools.partial(tiles_kernel, last), grid_spec=pltpu.Pre...  30.5 us

profile of v2, /device:TPU:0, one launch (start us, length us, event | category | flops | bytes accessed | tf_op | source)
XLA Modules:
  0.0 300.4 jit_solution(5454235397552249004)
XLA Ops:
  1.3 104.8 %exchange.1 = (bf16[4,4,4,2,128,256]{5,4,3,2,1,0:T(8,128)(2,1)}, bf16[2048,256]{1,0:T(8,128)(2,1)}, s32[12,128]{1,0:T(8,128)}) custom-call(bf16[32,128,256]{2,1,0:T(8,128)(2,1)} %bitcast.12, s32[1,128]{1,0:T(1,128)} %refs_1_.1, bf16[16,256]{1,0:T(8,128)(2,1)} %refs_2_.2, s32[2048]{0:T(1024)} %place_ref.3), custom_call_target="tpu_custom_call" | custom-call | tf_op jit(solution)/shard_map/exchange/pallas_call | solution.py:427
  106.0 12.6 %sum_tiles.2 = f32[48,128,256]{2,1,0:T(8,128)} custom-call(s32[432]{0:T(512)} %rows_ref.3, s32[304]{0:T(512)} %cols_ref.3, s32[1]{0:T(128)S(6)} %copy.14.count_ref, s32[2048]{0:T(1024)} %place_ref.3, bf16[432,128,128]{2,1,0:T(8,128)(2,1)} %tiles_ref.3, bf16[32,128,256]{2,1,0:T(8,128)(2,1)} %bitcast.13, bf16[16,128,256]{2,1,0:T(8,128)(2,1)} %bitcast.18, ...), custom_call_target="tpu_custom_call" | custom-call | tf_op jit(solution)/shard_map/sum_tiles/pallas_call | solution.py:549
  118.6 120.6 %update_exchange.1 = (bf16[4,4,4,2,128,256]{5,4,3,2,1,0:T(8,128)(2,1)}, bf16[2048,256]{1,0:T(8,128)(2,1)}, bf16[32,128,256]{2,1,0:T(8,128)(2,1)}) custom-call(f32[192,2,16,256]{3,2,1,0:T(8,128)} %bitcast.9, s32[12,128]{1,0:T(8,128)} %get-tuple-element.14.refs_1_, bf16[2,256,2048]{2,1,0:T(8,128)(2,1)} %w1_ref.1, bf16[2,2048,256]{2,1,0:T(8,128)(2,1)} %w2_ref.1), custom_call_target="tpu_custom_call" | custom-call | tf_op jit(solution)/shard_map/update_exchange/pallas_call | solution.py:445
  239.2 17.9 %sum_tiles.3 = (f32[48,128,256]{2,1,0:T(8,128)}, f32[2048,256]{1,0:T(8,128)}) custom-call(s32[432]{0:T(512)} %rows_ref.3, s32[304]{0:T(512)} %cols_ref.3, s32[1]{0:T(128)S(6)} %copy.14.count_ref, s32[2048]{0:T(1024)} %place_ref.3, bf16[432,128,128]{2,1,0:T(8,128)(2,1)} %tiles_ref.3, bf16[32,128,256]{2,1,0:T(8,128)(2,1)} %get-tuple-element.15.x_ref, ...), custom_call_target="tpu_custom_call" | custom-call | tf_op jit(solution)/shard_map/sum_tiles/pallas_call | solution.py:549
  257.2 39.6 %update.1 = (bf16[32,128,256]{2,1,0:T(8,128)(2,1)}, bf16[16,256]{1,0:T(8,128)(2,1)}) custom-call(f32[192,2,16,256]{3,2,1,0:T(8,128)} %bitcast.14, f32[64,2,16,256]{3,2,1,0:T(8,128)} %bitcast.16, bf16[2,256,2048]{2,1,0:T(8,128)(2,1)} %w1_ref.1, bf16[2,2048,256]{2,1,0:T(8,128)(2,1)} %w2_ref.1), custom_call_target="tpu_custom_call" | custom-call | tf_op jit(solution)/shard_map/update/pallas_call | solution.py:624
  296.8 0.0 copy-start
  296.8 3.0 %copy.15 = bf16[4096,256]{1,0:T(8,128)(2,1)} copy(bf16[4096,256]{1,0:T(8,128)(2,1)} %bitcast.15) | data formatting | bytes 4194304
  299.8 0.0 copy-done
  299.8 0.6 copy.16
Async XLA Ops:
  296.8 3.1 %copy-start = (bf16[16,256]{1,0:T(8,128)(2,1)S(1)}, bf16[16,256]{1,0:T(8,128)(2,1)}, u32[]{:S(2)}) copy-start(bf16[16,256]{1,0:T(8,128)(2,1)} %get-tuple-element.25) | copy-start | bytes 24580

commit v3 on v2

--- a/solution.py
+++ b/solution.py
@@ -7,7 +7,7 @@
 from jax.experimental.pallas import tpu as pltpu
 
 MESH = pl.DeviceIdType.MESH
-ROWS = ((0, 48), (48, 48), (96, 32))
+PARTS = ((0, 88, 0, 128), (0, 88, 128, 128), (88, 40, 0, 256))
 epsilon = 1e-06
 
 
@@ -28,10 +28,10 @@
 
 def exchange_kernel(fused, CH, *refs):
     if fused:
-        u_ref, lists, w1_ref, w2_ref, in_ref, hubs_ref, x_ref = refs[:7]
-        first_ref, second_ref, hidden_ref, normed_ref, w_sem = refs[7:12]
-        sum_refs = refs[12:23]
-        refs = refs[23:]
+        far_ref, lists, w1_ref, w2_ref, in_ref, hubs_ref, x_ref = refs[:7]
+        u_ref, u_sem, first_ref, second_ref, hidden_ref, normed_ref, w_sem = refs[7:14]
+        sum_refs = refs[14:25]
+        refs = refs[25:]
     else:
         x_ref, list_ref, hub_ref, place_ref, in_ref, hubs_ref, near_ref, lists, wide, ordered = refs[:10]
         refs = refs[10:]
@@ -42,6 +42,7 @@
                     list_sem, list_send, smem_sem, ag_send, ag_recv, p2_send, p2_recv, p3_send, p3_recv, local_sem, hub_send, hub_recv):
     x_ref, in_ref, hubs_ref, lists = given["x_ref"], given["in_ref"], given["hubs_ref"], given["lists"]
     if fused:
+        sums_in = load_sums(given["far_ref"], given["far_ref"], given["u_ref"], given["u_sem"])
         weights = load_weights(given["w1_ref"], given["w2_ref"], given["first_ref"], given["second_ref"], given["w_sem"], 0)
     else:
         list_ref, hub_ref, place_ref, near_ref = given["list_ref"], given["hub_ref"], given["place_ref"], given["near_ref"]
@@ -85,10 +86,10 @@
             hub_copy(step, off).wait()
 
     def ag_copy(p, q, direction):
-        lo, n = ROWS[p]
+        lo, n, left, lanes = PARTS[p]
         off = 1 if direction == 0 else 3
         seen = 4 - off
-        return remote(x_ref.at[pl.ds(q * per, per), pl.ds(lo, n)], tabs[p][seen - 1].at[pl.ds(q * per, per)],
+        return remote(x_ref.at[pl.ds(q * per, per), pl.ds(lo, n), pl.ds(left, lanes)], tabs[p][seen - 1].at[pl.ds(q * per, per)],
                       ag_send.at[p, q, direction], ag_recv.at[p, q, seen - 1], to(moved(co, p, off), core))
 
     def relay_copy(p, q):
@@ -108,7 +109,7 @@
             relay_copy(p, q).start()
 
     def assemble(p, i, js):
-        lo, n = ROWS[p]
+        lo, n, left, lanes = PARTS[p]
         d1, d2 = (p + 1) % 3, (p + 2) % 3
         where = lax.rem(co[p] + i, 4)
         row = 0 if i == 0 else p * 4 + i
@@ -117,7 +118,7 @@
                 k, flip = m // 2, lax.rem(m, 2)
                 target = device_of(moved(moved(co, d1, j), d2, k), flip)
                 b = lists[row, target]
-                value = x_ref[b, lo:lo + n, :] if i == 0 else tabs[p][i - 1][b]
+                value = x_ref[b, lo:lo + n, left:left + lanes] if i == 0 else tabs[p][i - 1][b]
                 stage[p][j, k, flip, where] = value
                 return carry
             lax.fori_loop(0, 8, piece, 0)
@@ -132,12 +133,15 @@
         for j in (1, 3, 2):
             p2_copy(p, i, j).start()
 
+    def pick(p, i):
+        for q in range(CH):
+            if i == 2 or (i == 1 and q % 2 == 0) or (i == 3 and q % 2 == 1):
+                ag_wait(ag_recv, tabs, p, q, i - 1, per)
+        assemble(p, i, (1, 3, 2, 0))
+
     def pass_on(i):
         for p in range(3):
-            for q in range(CH):
-                if i == 2 or (i == 1 and q % 2 == 0) or (i == 3 and q % 2 == 1):
-                    ag_wait(ag_recv, tabs, p, q, i - 1, per)
-            assemble(p, i, (1, 3, 2, 0))
+            pick(p, i)
             if p:
                 send2(p - 1, i)
         send2(2, i)
@@ -145,12 +149,12 @@
     place = ((0, 1, 2), (2, 0, 1), (1, 2, 0))
 
     def landing(p, s1, s2, s_core):
-        lo, n = ROWS[p]
+        lo, n, left, lanes = PARTS[p]
         idx = [None, None, None]
         idx[p] = slice(None)
         idx[(p + 1) % 3] = s1
         idx[(p + 2) % 3] = s2
-        return in_ref.at[idx[0], idx[1], idx[2], s_core, pl.ds(lo, n)]
+        return in_ref.at[idx[0], idx[1], idx[2], s_core, pl.ds(lo, n), pl.ds(left, lanes)]
 
     def p3_copy(p, j, k, flip):
         d1, d2 = (p + 1) % 3, (p + 2) % 3
@@ -175,50 +179,67 @@
     def own_pass():
         for p in range(3):
             assemble(p, 0, (1, 3, 2, 0))
-            if fused and p == 0:
-                ag_start(CH - 1)
             if p:
                 send2(p - 1, 0)
         send2(2, 0)
 
     if fused:
-        sums = HubSum(co, core, remote, to, u_ref := given["u_ref"], *given["sum_refs"])
+        sums = HubSum(co, core, remote, to, given["u_ref"], *given["sum_refs"])
+        sums_in(STEPS)
         sums.start(0)
         weights()
         first_ref, second_ref = given["first_ref"], given["second_ref"]
         size = 4096 // CH
         for q in range(CH):
-            update_rows(u_ref, x_ref, q, size, first_ref, second_ref, given["hidden_ref"], given["normed_ref"])
+            sums_in(q)
+            update_rows(given["u_ref"], x_ref, q, size, first_ref, second_ref, given["hidden_ref"], given["normed_ref"])
+            if q == 2:
+                sums.start(1)
+            if q == 6:
+                sums.start(2)
             if q >= 1:
                 ag_start(q - 1)
-            if q == 2:
+            if q == 1:
                 sums.wait(0)
                 sums.add(0)
-            if q == 3:
-                sums.start(1)
+            if q == 5:
+                sums.wait(1)
+                sums.add(1)
             if q >= 4:
                 relay_on(q - 4)
-        own_pass()
-        sums.wait(1)
-        sums.add(1)
-        for q in range(CH - 4, CH):
-            relay_on(q)
-            if q == CH - 3:
-                sums.start(2)
-        pass_on(1)
+        assemble(0, 0, (1, 3, 2, 0))
+        ag_start(CH - 1)
+        relay_on(CH - 4)
+        assemble(1, 0, (1, 3, 2, 0))
         sums.wait(2)
         sums.add(2)
-        pass_on(3)
+        relay_on(CH - 3)
+        assemble(2, 0, (1, 3, 2, 0))
         sums.start(3)
-        pass_on(2)
+        relay_on(CH - 2)
+        for p in range(3):
+            send2(p, 0)
+        relay_on(CH - 1)
+        pick(0, 1)
+        pick(1, 1)
+        pick(2, 1)
         sums.wait(3)
         gathered[co[0], co[1], co[2], core] = feed_forward(sums.result(), first_ref, second_ref)
-        for p in range(3):
-            send3(p, 0)
+        pick(0, 3)
         hub_start(0)
-        finish(1)
+        for p in range(3):
+            send2(p, 1)
+        pick(1, 3)
+        send2(0, 3)
+        pick(2, 3)
+        send2(1, 3)
+        send2(2, 3)
+        pass_on(2)
         hub_wait(0)
         hub_start(1)
+        for p in range(3):
+            send3(p, 0)
+        finish(1)
         finish(3)
         hub_wait(1)
         hub_start(2)
@@ -306,6 +327,20 @@
     pltpu.make_async_copy(ref, ref, sem.at[p, i, slot]).wait()
 
 
+STEPS = 8
+
+
+def load_sums(far_ref, part_ref, u_ref, sem):
+    rows = 128 // STEPS
+    copies = [pltpu.make_async_copy(far_ref.at[pl.ds(64 + q * rows, rows)], u_ref.at[pl.ds(64 + q * rows, rows)], sem.at[q]) for q in range(STEPS)]
+    copies.append(pltpu.make_async_copy(part_ref.at[pl.ds(0, 64)], u_ref.at[pl.ds(0, 64)], sem.at[STEPS]))
+    copies[0].start()
+    copies[STEPS].start()
+    for q in range(1, STEPS):
+        copies[q].start()
+    return lambda q: copies[q].wait()
+
+
 def load_weights(w1_ref, w2_ref, first_ref, second_ref, sem, layer):
     copies = [
         pltpu.make_async_copy(w1_ref.at[layer], first_ref, sem.at[0]),
@@ -395,7 +430,7 @@
 
 def weight_scratch(size):
     bf = jnp.bfloat16
-    return [pltpu.VMEM((256, 2048), bf), pltpu.VMEM((2048, 256), bf), pltpu.VMEM((size, 2048), bf), pltpu.VMEM((size, 256), bf), pltpu.SemaphoreType.DMA((2,))]
+    return [pltpu.VMEM((192, 2, 16, 256), jnp.float32), pltpu.SemaphoreType.DMA((STEPS + 1,)), pltpu.VMEM((256, 2048), bf), pltpu.VMEM((2048, 256), bf), pltpu.VMEM((size, 2048), bf), pltpu.VMEM((size, 256), bf), pltpu.SemaphoreType.DMA((2,))]
 
 
 def update_rows(u_ref, x_ref, q, size, first, second, hidden_ref, normed_ref):
@@ -414,9 +449,9 @@
 def route_scratch(chunks):
     bf, D = jnp.bfloat16, pltpu.SemaphoreType.DMA
     scratch = [pltpu.VMEM((4, 4, 4, 2, 16, 256), bf)]
-    scratch += [pltpu.VMEM((32, n, 256), bf) for lo, n in ROWS for _ in range(3)]
-    scratch += [pltpu.VMEM((4, 4, 2, 4, n, 256), bf) for lo, n in ROWS]
-    scratch += [pltpu.VMEM((3, 4, 2, 4, n, 256), bf) for lo, n in ROWS]
+    scratch += [pltpu.VMEM((32, n, w), bf) for lo, n, left, w in PARTS for _ in range(3)]
+    scratch += [pltpu.VMEM((4, 4, 2, 4, n, w), bf) for lo, n, left, w in PARTS]
+    scratch += [pltpu.VMEM((3, 4, 2, 4, n, w), bf) for lo, n, left, w in PARTS]
     scratch += [D((3, 4)), D((3, 4)), D, D((3, chunks, 3)), D((3, chunks, 3)), D((3, 4, 3)), D((3, 4, 3)), D((3, 4, 8)), D((3, 4, 8)), D((12,))]
     return scratch + [D((4, 3)), D((4, 3))]
 
@@ -449,7 +484,7 @@
             jax.ShapeDtypeStruct((2048, 256), bf),
             jax.ShapeDtypeStruct((32, 128, 256), bf),
         ),
-        in_specs=[V, pl.BlockSpec(memory_space=pltpu.SMEM), A, A],
+        in_specs=[A, pl.BlockSpec(memory_space=pltpu.SMEM), A, A],
         out_specs=(pl.BlockSpec(memory_space=pltpu.HBM), V, V),
         scratch_shapes=weight_scratch(512) + sum_scratch() + route_scratch(8),
         compiler_params=pltpu.CompilerParams(collective_id=1, has_side_effects=True, vmem_limit_bytes=60 * 2**20),
@@ -578,7 +613,8 @@
     return total.astype(jnp.bfloat16)
 
 
-def update_kernel(u_ref, part_ref, w1_ref, w2_ref, out_ref, hub_out_ref, first_ref, second_ref, hidden_ref, normed_ref, w_sem, *sum_refs):
+def update_kernel(far_ref, part_ref, w1_ref, w2_ref, out_ref, hub_out_ref, u_ref, u_sem, first_ref, second_ref, hidden_ref, normed_ref, w_sem, *sum_refs):
+    sums_in = load_sums(far_ref, part_ref, u_ref, u_sem)
     weights = load_weights(w1_ref, w2_ref, first_ref, second_ref, w_sem, 1)
     co, core = coords()
 
@@ -595,16 +631,18 @@
     def remote(src, dst, ssem, rsem, dev):
         return pltpu.make_async_remote_copy(src_ref=src, dst_ref=dst, send_sem=ssem, recv_sem=rsem, device_id=dev, device_id_type=MESH)
 
-    sums = HubSum(co, core, remote, to, part_ref, *sum_refs)
+    sums = HubSum(co, core, remote, to, u_ref, *sum_refs)
+    sums_in(STEPS)
     sums.start(0)
     weights()
     size = hidden_ref.shape[0]
-    for q in range(4096 // size):
+    for q in range(STEPS):
+        sums_in(q)
         update_rows(u_ref, out_ref, q, size, first_ref, second_ref, hidden_ref, normed_ref)
-        if q == 1:
+        if q == 0:
             sums.wait(0)
             sums.add(0)
-        if q == 2:
+        if q == 1:
             sums.start(1)
         if q == 5:
             sums.wait(1)
@@ -624,7 +662,7 @@
     return pl.pallas_call(
         update_kernel,
         out_shape=(jax.ShapeDtypeStruct((32, 128, 256), bf), jax.ShapeDtypeStruct((16, 256), bf)),
-        in_specs=[V, V, A, A],
+        in_specs=[A, A, A, A],
         out_specs=(V, V),
         scratch_shapes=weight_scratch(512) + sum_scratch(),
         compiler_params=pltpu.CompilerParams(collective_id=2, has_side_effects=True, vmem_limit_bytes=60 * 2**20),

time: 299 us -> 289 us (0.967)
  Pallas kernels: 295 us -> 284 us
    pallas_call x1, Pallas kernels: 39.6 us -> 34 us  [update(): pl.pallas_call(update_kernel, out_shape=(jax.ShapeDtypeStruct((32, 128, 2...]
    pallas_call x1, Pallas kernels: 121 us -> 117 us  [update_exchange(): pl.pallas_call(functools.partial(exchange_kernel, True, 8), out_shape=(ja...]
where the time goes in v3:
time: 289 us
  Pallas kernels  284 us (98%)
  local copies, waits for them, and re-layouts  3.65 us (1%)
    pallas_call x1, Pallas kernels, update_exchange(): pl.pallas_call(functools.partial(exchange_kernel, True, 8), out_shape=(ja...  117 us
    pallas_call x1, Pallas kernels, exchange(): pl.pallas_call(functools.partial(exchange_kernel, False, 4), out_shape=(j...  102 us
    pallas_call x1, Pallas kernels, update(): pl.pallas_call(update_kernel, out_shape=(jax.ShapeDtypeStruct((32, 128, 2...  34 us
    pallas_call x2, Pallas kernels, sum_tiles(): pl.pallas_call(functools.partial(tiles_kernel, last), grid_spec=pltpu.Pre...  30.9 us

profile of v3, /device:TPU:0, one launch (start us, length us, event | category | flops | bytes accessed | tf_op | source)
XLA Modules:
  0.0 289.0 jit_solution(7312068260580745842)
XLA Ops:
  1.3 102.5 %exchange.1 = (bf16[4,4,4,2,128,256]{5,4,3,2,1,0:T(8,128)(2,1)}, bf16[2048,256]{1,0:T(8,128)(2,1)}, s32[12,128]{1,0:T(8,128)}) custom-call(bf16[32,128,256]{2,1,0:T(8,128)(2,1)} %bitcast.12, s32[1,128]{1,0:T(1,128)} %refs_1_.1, bf16[16,256]{1,0:T(8,128)(2,1)} %refs_2_.2, s32[2048]{0:T(1024)} %place_ref.3), custom_call_target="tpu_custom_call" | custom-call | tf_op jit(solution)/shard_map/exchange/pallas_call | solution.py:462
  103.8 12.8 %sum_tiles.2 = f32[48,128,256]{2,1,0:T(8,128)} custom-call(s32[432]{0:T(512)} %rows_ref.3, s32[304]{0:T(512)} %cols_ref.3, s32[1]{0:T(128)S(6)} %copy.14.count_ref, s32[2048]{0:T(1024)} %place_ref.3, bf16[432,128,128]{2,1,0:T(8,128)(2,1)} %tiles_ref.3, bf16[32,128,256]{2,1,0:T(8,128)(2,1)} %bitcast.13, bf16[16,128,256]{2,1,0:T(8,128)(2,1)} %bitcast.18, ...), custom_call_target="tpu_custom_call" | custom-call | tf_op jit(solution)/shard_map/sum_tiles/pallas_call | solution.py:584
  116.6 116.6 %update_exchange.1 = (bf16[4,4,4,2,128,256]{5,4,3,2,1,0:T(8,128)(2,1)}, bf16[2048,256]{1,0:T(8,128)(2,1)}, bf16[32,128,256]{2,1,0:T(8,128)(2,1)}) custom-call(f32[192,2,16,256]{3,2,1,0:T(8,128)} %bitcast.9, s32[12,128]{1,0:T(8,128)} %get-tuple-element.14.refs_1_, bf16[2,256,2048]{2,1,0:T(8,128)(2,1)} %w1_ref.1, bf16[2,2048,256]{2,1,0:T(8,128)(2,1)} %w2_ref.1), custom_call_target="tpu_custom_call" | custom-call | tf_op jit(solution)/shard_map/update_exchange/pallas_call | solution.py:480
  233.2 18.0 %sum_tiles.3 = (f32[48,128,256]{2,1,0:T(8,128)}, f32[2048,256]{1,0:T(8,128)}) custom-call(s32[432]{0:T(512)} %rows_ref.3, s32[304]{0:T(512)} %cols_ref.3, s32[1]{0:T(128)S(6)} %copy.14.count_ref, s32[2048]{0:T(1024)} %place_ref.3, bf16[432,128,128]{2,1,0:T(8,128)(2,1)} %tiles_ref.3, bf16[32,128,256]{2,1,0:T(8,128)(2,1)} %get-tuple-element.15.x_ref, ...), custom_call_target="tpu_custom_call" | custom-call | tf_op jit(solution)/shard_map/sum_tiles/pallas_call | solution.py:584
  251.3 34.0 %update.1 = (bf16[32,128,256]{2,1,0:T(8,128)(2,1)}, bf16[16,256]{1,0:T(8,128)(2,1)}) custom-call(f32[192,2,16,256]{3,2,1,0:T(8,128)} %bitcast.14, f32[64,2,16,256]{3,2,1,0:T(8,128)} %bitcast.16, bf16[2,256,2048]{2,1,0:T(8,128)(2,1)} %w1_ref.1, bf16[2,2048,256]{2,1,0:T(8,128)(2,1)} %w2_ref.1), custom_call_target="tpu_custom_call" | custom-call | tf_op jit(solution)/shard_map/update/pallas_call | solution.py:662
  285.3 0.0 copy-start
  285.3 3.0 %copy.15 = bf16[4096,256]{1,0:T(8,128)(2,1)} copy(bf16[4096,256]{1,0:T(8,128)(2,1)} %bitcast.15) | data formatting | bytes 4194304
  288.4 0.0 copy-done
  288.4 0.6 copy.16
Async XLA Ops:
  285.3 3.1 %copy-start = (bf16[16,256]{1,0:T(8,128)(2,1)S(1)}, bf16[16,256]{1,0:T(8,128)(2,1)}, u32[]{:S(2)}) copy-start(bf16[16,256]{1,0:T(8,128)(2,1)} %get-tuple-element.25) | copy-start | bytes 24580

commit v4 on v3

--- a/solution.py
+++ b/solution.py
@@ -73,16 +73,21 @@
         if step == 3:
             part = gathered.at[:, :, :, core]
             return remote(part, part, hub_send.at[3, 0], hub_recv.at[3, 0], to(co, 1 - core))
-        dim = 2 - step
-        part = (gathered.at[co[0], co[1], co[2], core], gathered.at[co[0], co[1], :, core], gathered.at[co[0], :, :, core])[step]
-        return remote(part, part, hub_send.at[step, off - 1], hub_recv.at[step, 3 - off], to(moved(co, dim, off), core))
+        half, off = off // 4, off % 4
+        rows = pl.ds(half * 8, 8)
+        dim = ((2, 1, 0), (0, 2, 1))[half][step]
+        x, y, z = co
+        every = slice(None)
+        at = (((x, y, z), (x, y, every), (x, every, every)), ((x, y, z), (every, y, z), (every, y, every)))[half][step]
+        part = gathered.at[at[0], at[1], at[2], core, rows]
+        return remote(part, part, hub_send.at[step, half * 3 + off - 1], hub_recv.at[step, half * 3 + 3 - off], to(moved(co, dim, off), core))
 
     def hub_start(step):
-        for off in (1, 2, 3) if step < 3 else (1,):
+        for off in (1, 2, 3, 5, 6, 7) if step < 3 else (1,):
             hub_copy(step, off).start()
 
     def hub_wait(step):
-        for off in (1, 2, 3) if step < 3 else (1,):
+        for off in (1, 2, 3, 5, 6, 7) if step < 3 else (1,):
             hub_copy(step, off).wait()
 
     def ag_copy(p, q, direction):
@@ -453,7 +458,7 @@
     scratch += [pltpu.VMEM((4, 4, 2, 4, n, w), bf) for lo, n, left, w in PARTS]
     scratch += [pltpu.VMEM((3, 4, 2, 4, n, w), bf) for lo, n, left, w in PARTS]
     scratch += [D((3, 4)), D((3, 4)), D, D((3, chunks, 3)), D((3, chunks, 3)), D((3, 4, 3)), D((3, 4, 3)), D((3, 4, 8)), D((3, 4, 8)), D((12,))]
-    return scratch + [D((4, 3)), D((4, 3))]
+    return scratch + [D((4, 6)), D((4, 6))]
 
 
 def exchange(x, send_list, hubs, place):

time: 289 us -> 287 us (level)
    pallas_call x2, Pallas kernels: 30.9 us -> 34.5 us  [sum_tiles(): pl.pallas_call(functools.partial(tiles_kernel, last), grid_spec=pltpu.Pre...]
where the time goes in v4:
time: 287 us
  Pallas kernels  282 us (98%)
  local copies, waits for them, and re-layouts  3.65 us (1%)
    pallas_call x1, Pallas kernels, update_exchange(): pl.pallas_call(functools.partial(exchange_kernel, True, 8), out_shape=(ja...  114 us
    pallas_call x1, Pallas kernels, exchange(): pl.pallas_call(functools.partial(exchange_kernel, False, 4), out_shape=(j...  101 us
    pallas_call x2, Pallas kernels, sum_tiles(): pl.pallas_call(functools.partial(tiles_kernel, last), grid_spec=pltpu.Pre...  34.5 us
    pallas_call x1, Pallas kernels, update(): pl.pallas_call(update_kernel, out_shape=(jax.ShapeDtypeStruct((32, 128, 2...  32.9 us

profile of v4, /device:TPU:0, one launch (start us, length us, event | category | flops | bytes accessed | tf_op | source)
XLA Modules:
  0.0 286.8 jit_solution(13020436184626612719)
XLA Ops:
  1.3 100.7 %exchange.1 = (bf16[4,4,4,2,128,256]{5,4,3,2,1,0:T(8,128)(2,1)}, bf16[2048,256]{1,0:T(8,128)(2,1)}, s32[12,128]{1,0:T(8,128)}) custom-call(bf16[32,128,256]{2,1,0:T(8,128)(2,1)} %bitcast.12, s32[1,128]{1,0:T(1,128)} %refs_1_.1, bf16[16,256]{1,0:T(8,128)(2,1)} %refs_2_.2, s32[2048]{0:T(1024)} %place_ref.3), custom_call_target="tpu_custom_call" | custom-call | tf_op jit(solution)/shard_map/exchange/pallas_call | solution.py:467
  101.9 14.7 %sum_tiles.2 = f32[48,128,256]{2,1,0:T(8,128)} custom-call(s32[432]{0:T(512)} %rows_ref.3, s32[304]{0:T(512)} %cols_ref.3, s32[1]{0:T(128)S(6)} %copy.14.count_ref, s32[2048]{0:T(1024)} %place_ref.3, bf16[432,128,128]{2,1,0:T(8,128)(2,1)} %tiles_ref.3, bf16[32,128,256]{2,1,0:T(8,128)(2,1)} %bitcast.13, bf16[16,128,256]{2,1,0:T(8,128)(2,1)} %bitcast.18, ...), custom_call_target="tpu_custom_call" | custom-call | tf_op jit(solution)/shard_map/sum_tiles/pallas_call | solution.py:589
  116.6 113.8 %update_exchange.1 = (bf16[4,4,4,2,128,256]{5,4,3,2,1,0:T(8,128)(2,1)}, bf16[2048,256]{1,0:T(8,128)(2,1)}, bf16[32,128,256]{2,1,0:T(8,128)(2,1)}) custom-call(f32[192,2,16,256]{3,2,1,0:T(8,128)} %bitcast.9, s32[12,128]{1,0:T(8,128)} %get-tuple-element.14.refs_1_, bf16[2,256,2048]{2,1,0:T(8,128)(2,1)} %w1_ref.1, bf16[2,2048,256]{2,1,0:T(8,128)(2,1)} %w2_ref.1), custom_call_target="tpu_custom_call" | custom-call | tf_op jit(solution)/shard_map/update_exchange/pallas_call | solution.py:485
  230.4 19.8 %sum_tiles.3 = (f32[48,128,256]{2,1,0:T(8,128)}, f32[2048,256]{1,0:T(8,128)}) custom-call(s32[432]{0:T(512)} %rows_ref.3, s32[304]{0:T(512)} %cols_ref.3, s32[1]{0:T(128)S(6)} %copy.14.count_ref, s32[2048]{0:T(1024)} %place_ref.3, bf16[432,128,128]{2,1,0:T(8,128)(2,1)} %tiles_ref.3, bf16[32,128,256]{2,1,0:T(8,128)(2,1)} %get-tuple-element.15.x_ref, ...), custom_call_target="tpu_custom_call" | custom-call | tf_op jit(solution)/shard_map/sum_tiles/pallas_call | solution.py:589
  250.2 32.9 %update.1 = (bf16[32,128,256]{2,1,0:T(8,128)(2,1)}, bf16[16,256]{1,0:T(8,128)(2,1)}) custom-call(f32[192,2,16,256]{3,2,1,0:T(8,128)} %bitcast.14, f32[64,2,16,256]{3,2,1,0:T(8,128)} %bitcast.16, bf16[2,256,2048]{2,1,0:T(8,128)(2,1)} %w1_ref.1, bf16[2,2048,256]{2,1,0:T(8,128)(2,1)} %w2_ref.1), custom_call_target="tpu_custom_call" | custom-call | tf_op jit(solution)/shard_map/update/pallas_call | solution.py:667
  283.1 0.0 copy-start
  283.1 3.0 %copy.15 = bf16[4096,256]{1,0:T(8,128)(2,1)} copy(bf16[4096,256]{1,0:T(8,128)(2,1)} %bitcast.15) | data formatting | bytes 4194304
  286.2 0.0 copy-done
  286.2 0.6 copy.16
Async XLA Ops:
  283.1 3.1 %copy-start = (bf16[16,256]{1,0:T(8,128)(2,1)S(1)}, bf16[16,256]{1,0:T(8,128)(2,1)}, u32[]{:S(2)}) copy-start(bf16[16,256]{1,0:T(8,128)(2,1)} %get-tuple-element.25) | copy-start | bytes 24580

commit v5 on v4

--- a/solution.py
+++ b/solution.py
@@ -652,7 +652,6 @@
         if q == 5:
             sums.wait(1)
             sums.add(1)
-        if q == 6:
             sums.start(2)
     sums.wait(2)
     sums.add(2)

time: 287 us -> 285 us (level)
  no operation moved by 1% of the time
where the time goes in v5:
time: 285 us
  Pallas kernels  280 us (98%)
  local copies, waits for them, and re-layouts  3.65 us (1%)
    pallas_call x1, Pallas kernels, update_exchange(): pl.pallas_call(functools.partial(exchange_kernel, True, 8), out_shape=(ja...  115 us
    pallas_call x1, Pallas kernels, exchange(): pl.pallas_call(functools.partial(exchange_kernel, False, 4), out_shape=(j...  101 us
    pallas_call x2, Pallas kernels, sum_tiles(): pl.pallas_call(functools.partial(tiles_kernel, last), grid_spec=pltpu.Pre...  33.6 us
    pallas_call x1, Pallas kernels, update(): pl.pallas_call(update_kernel, out_shape=(jax.ShapeDtypeStruct((32, 128, 2...  30.7 us

profile of v5, /device:TPU:0, one launch (start us, length us, event | category | flops | bytes accessed | tf_op | source)
XLA Modules:
  0.0 284.6 jit_solution(17235931438656056353)
XLA Ops:
  1.3 100.7 %exchange.1 = (bf16[4,4,4,2,128,256]{5,4,3,2,1,0:T(8,128)(2,1)}, bf16[2048,256]{1,0:T(8,128)(2,1)}, s32[12,128]{1,0:T(8,128)}) custom-call(bf16[32,128,256]{2,1,0:T(8,128)(2,1)} %bitcast.12, s32[1,128]{1,0:T(1,128)} %refs_1_.1, bf16[16,256]{1,0:T(8,128)(2,1)} %refs_2_.2, s32[2048]{0:T(1024)} %place_ref.3), custom_call_target="tpu_custom_call" | custom-call | tf_op jit(solution)/shard_map/exchange/pallas_call | solution.py:467
  101.9 14.2 %sum_tiles.2 = f32[48,128,256]{2,1,0:T(8,128)} custom-call(s32[432]{0:T(512)} %rows_ref.3, s32[304]{0:T(512)} %cols_ref.3, s32[1]{0:T(128)S(6)} %copy.14.count_ref, s32[2048]{0:T(1024)} %place_ref.3, bf16[432,128,128]{2,1,0:T(8,128)(2,1)} %tiles_ref.3, bf16[32,128,256]{2,1,0:T(8,128)(2,1)} %bitcast.13, bf16[16,128,256]{2,1,0:T(8,128)(2,1)} %bitcast.18, ...), custom_call_target="tpu_custom_call" | custom-call | tf_op jit(solution)/shard_map/sum_tiles/pallas_call | solution.py:589
  116.2 114.7 %update_exchange.1 = (bf16[4,4,4,2,128,256]{5,4,3,2,1,0:T(8,128)(2,1)}, bf16[2048,256]{1,0:T(8,128)(2,1)}, bf16[32,128,256]{2,1,0:T(8,128)(2,1)}) custom-call(f32[192,2,16,256]{3,2,1,0:T(8,128)} %bitcast.9, s32[12,128]{1,0:T(8,128)} %get-tuple-element.14.refs_1_, bf16[2,256,2048]{2,1,0:T(8,128)(2,1)} %w1_ref.1, bf16[2,2048,256]{2,1,0:T(8,128)(2,1)} %w2_ref.1), custom_call_target="tpu_custom_call" | custom-call | tf_op jit(solution)/shard_map/update_exchange/pallas_call | solution.py:485
  230.8 19.4 %sum_tiles.3 = (f32[48,128,256]{2,1,0:T(8,128)}, f32[2048,256]{1,0:T(8,128)}) custom-call(s32[432]{0:T(512)} %rows_ref.3, s32[304]{0:T(512)} %cols_ref.3, s32[1]{0:T(128)S(6)} %copy.14.count_ref, s32[2048]{0:T(1024)} %place_ref.3, bf16[432,128,128]{2,1,0:T(8,128)(2,1)} %tiles_ref.3, bf16[32,128,256]{2,1,0:T(8,128)(2,1)} %get-tuple-element.15.x_ref, ...), custom_call_target="tpu_custom_call" | custom-call | tf_op jit(solution)/shard_map/sum_tiles/pallas_call | solution.py:589
  250.2 30.7 %update.1 = (bf16[32,128,256]{2,1,0:T(8,128)(2,1)}, bf16[16,256]{1,0:T(8,128)(2,1)}) custom-call(f32[192,2,16,256]{3,2,1,0:T(8,128)} %bitcast.14, f32[64,2,16,256]{3,2,1,0:T(8,128)} %bitcast.16, bf16[2,256,2048]{2,1,0:T(8,128)(2,1)} %w1_ref.1, bf16[2,2048,256]{2,1,0:T(8,128)(2,1)} %w2_ref.1), custom_call_target="tpu_custom_call" | custom-call | tf_op jit(solution)/shard_map/update/pallas_call | solution.py:666
  281.0 0.0 copy-start
  281.0 3.0 %copy.15 = bf16[4096,256]{1,0:T(8,128)(2,1)} copy(bf16[4096,256]{1,0:T(8,128)(2,1)} %bitcast.15) | data formatting | bytes 4194304
  284.0 0.0 copy-done
  284.0 0.6 copy.16
Async XLA Ops:
  281.0 3.1 %copy-start = (bf16[16,256]{1,0:T(8,128)(2,1)S(1)}, bf16[16,256]{1,0:T(8,128)(2,1)}, u32[]{:S(2)}) copy-start(bf16[16,256]{1,0:T(8,128)(2,1)} %get-tuple-element.25) | copy-start | bytes 24580
